TPU v7x, 256 devices: a whole 4x4x8 slice. The times are simulated.
256 devices in a mesh: section: 8 (over y, core), dp: 32 (over x, z).
Axes of the slice: x: 4, y: 4, z: 8, core: 2. Of those that a mesh axis runs over, the one named last changes fastest.
Arguments:
- tokens: bfloat16 [4096, 8192], P('dp'), may hold values from -6 to 6
- cotangent: bfloat16 [4096, 8192], P('dp'), may hold values from -9 to 9
- down_weight: bfloat16 [8, 8192, 256], P('section', 'dp'), may hold values from -0.0625 to 0.0625
- up_weight: bfloat16 [8, 8192, 256], P('section', 'dp'), may hold values from -0.0625 to 0.0625
- norm_gain: float32 [8, 8192], P('section'), may hold values from 0.5 to 1.5
- lengths: int32 [32, 4], P('dp'), may hold values from 1 to 96, 128 in all within a row
Outputs:
- fisher: float32 [8, 8192, 256], P('section', 'dp')
Inputs may be any that keep to these rules, and one draw needn't show every extreme that they name: Each replica's 4 lengths sum to 128, and the longest in each replica is exactly 96.
All inputs are finite; a program needn't handle non-finite values.
Results may differ from a plain program's by a relative error of at most 0.0039.
Values may be sent and summed in bfloat16 or wider, within the bound.
A program may use at most 64 MiB of HBM per device.

v0:
```python
import jax
import jax.numpy as jnp
from jax import lax
from jax.sharding import Mesh
from jax.sharding import PartitionSpec as P

MICRO = 8
DP = ("dp_0", "dp_1")


epsilon = 1e-05


def side_by_side(arrays, axis, dim, along):
    ends, at = ([], 0)
    for a in arrays[:-1]:
        at += a.shape[along]
        ends.append(at)
    both = jnp.concatenate(arrays, axis=along)
    return tuple(jnp.split(lax.all_gather(both, axis, axis=dim, tiled=True), ends, axis=along))


def from_behind(array, axis, by):
    peers = lax.axis_size(axis)
    pairs = [(i, i + by) for i in range(peers) if 0 <= i + by < peers]
    return lax.ppermute(array, axis, pairs)


def sum_by_axis(array, axes, dim):
    for axis in axes:
        array = lax.psum_scatter(array, axis, scatter_dimension=dim, tiled=True)
    return array


def layer_forward(inputs, gain_row, w_down, w_up):
    wide_rows = inputs.astype(jnp.float32)
    inverse_rms = lax.rsqrt(jnp.mean(wide_rows * wide_rows, axis=-1, keepdims=True) + epsilon)
    normed = (wide_rows * inverse_rms * gain_row).astype(jnp.bfloat16)
    pre_act = jnp.dot(normed, w_down, preferred_element_type=jnp.float32)
    activated = jax.nn.silu(pre_act).astype(jnp.bfloat16)
    branch = lax.dot_general(
        activated, w_up, (((1,), (1,)), ((), ())), preferred_element_type=jnp.float32
    )
    return (wide_rows + branch).astype(jnp.bfloat16)


def layer_backward(inputs, upstream, gain_row, w_down, w_up):
    wide_rows = inputs.astype(jnp.float32)
    inverse_rms = lax.rsqrt(jnp.mean(wide_rows * wide_rows, axis=-1, keepdims=True) + epsilon)
    normed = (wide_rows * inverse_rms * gain_row).astype(jnp.bfloat16)
    pre_act = jnp.dot(normed, w_down, preferred_element_type=jnp.float32)
    act_grad = jnp.dot(upstream, w_up, preferred_element_type=jnp.float32)
    sigmoid_z = jax.nn.sigmoid(pre_act)
    pre_grad = (act_grad * sigmoid_z * (1.0 + pre_act * (1.0 - sigmoid_z))).astype(jnp.bfloat16)
    norm_grad = lax.dot_general(
        pre_grad, w_down, (((1,), (1,)), ((), ())), preferred_element_type=jnp.float32
    )
    gained = norm_grad * gain_row
    inner = jnp.mean(wide_rows * gained, axis=-1, keepdims=True)
    input_grad = upstream.astype(jnp.float32) + inverse_rms * (
        gained - wide_rows * inverse_rms * inverse_rms * inner
    )
    return (input_grad.astype(jnp.bfloat16), normed, pre_grad)


def replica_squares(norm_rows, grad_rows, seq_lengths):
    row_ids = jnp.arange(norm_rows.shape[0], dtype=jnp.int32)
    ends = jnp.cumsum(seq_lengths)
    starts = ends - seq_lengths
    fisher_sum = jnp.zeros((norm_rows.shape[1], grad_rows.shape[1]), jnp.float32)
    for seq_index in range(seq_lengths.shape[0]):
        inside = (row_ids >= starts[seq_index]) & (row_ids < ends[seq_index])
        masked = jnp.where(inside[:, None], grad_rows, jnp.zeros_like(grad_rows))
        seq_grad = lax.dot_general(
            norm_rows, masked, (((0,), (0,)), ((), ())), preferred_element_type=jnp.float32
        )
        fisher_sum = fisher_sum + seq_grad * seq_grad
    return fisher_sum


def per_device(tokens, cotangent, down_weight, up_weight, norm_gain, lengths):
    gathered = side_by_side((down_weight, up_weight), DP, 1, 0)
    w_down = gathered[0][0]
    w_up = gathered[1][0]
    gain_row = norm_gain[0]
    section_count = lax.axis_size("section")
    section_index = lax.axis_index("section")
    row_count = tokens.shape[0]
    width = tokens.shape[1]
    hidden_width = w_down.shape[1]
    micro_rows = row_count // MICRO
    tick_count = MICRO + section_count - 1

    def forward_tick(moment, state_now):
        incoming, stored_inputs = state_now
        micro_index = moment - section_index
        active = (micro_index >= 0) & (micro_index < MICRO)
        begin_row = jnp.clip(micro_index, 0, MICRO - 1) * micro_rows
        first_rows = lax.dynamic_slice_in_dim(tokens, begin_row, micro_rows, 0)
        entering = jnp.where(section_index == 0, first_rows, incoming)

        def forward_compute_tick(operands):
            updated = lax.dynamic_update_slice_in_dim(operands[1], operands[0], begin_row, 0)
            return (layer_forward(operands[0], gain_row, w_down, w_up), updated)

        def forward_no_work(operands):
            return (jnp.zeros_like(operands[0]), operands[1])

        leaving, stored_inputs = lax.cond(
            active, forward_compute_tick, forward_no_work, (entering, stored_inputs)
        )
        return (from_behind(leaving, "section", 1), stored_inputs)

    start_state = (
        jnp.zeros((micro_rows, width), jnp.bfloat16),
        jnp.zeros((row_count, width), jnp.bfloat16),
    )
    stored_inputs = lax.fori_loop(0, tick_count, forward_tick, start_state)[1]

    def backward_tick(moment, state_now):
        incoming, norm_rows, grad_rows = state_now
        micro_index = moment - (section_count - 1 - section_index)
        active = (micro_index >= 0) & (micro_index < MICRO)
        begin_row = jnp.clip(micro_index, 0, MICRO - 1) * micro_rows
        last_rows = lax.dynamic_slice_in_dim(cotangent, begin_row, micro_rows, 0)
        entering = jnp.where(section_index == section_count - 1, last_rows, incoming)

        def backward_compute_tick(operands):
            layer_input = lax.dynamic_slice_in_dim(stored_inputs, begin_row, micro_rows, 0)
            input_grad, normed, pre_grad = layer_backward(
                layer_input, operands[0], gain_row, w_down, w_up
            )
            norm_new = lax.dynamic_update_slice_in_dim(operands[1], normed, begin_row, 0)
            grad_new = lax.dynamic_update_slice_in_dim(operands[2], pre_grad, begin_row, 0)
            return (input_grad, norm_new, grad_new)

        def backward_no_work(operands):
            return (jnp.zeros_like(operands[0]), operands[1], operands[2])

        leaving, norm_rows, grad_rows = lax.cond(
            active, backward_compute_tick, backward_no_work, (entering, norm_rows, grad_rows)
        )
        return (from_behind(leaving, "section", -1), norm_rows, grad_rows)

    start_back = (
        jnp.zeros((micro_rows, width), jnp.bfloat16),
        jnp.zeros((row_count, width), jnp.bfloat16),
        jnp.zeros((row_count, hidden_width), jnp.bfloat16),
    )
    finished = lax.fori_loop(0, tick_count, backward_tick, start_back)
    norm_rows = finished[1]
    grad_rows = finished[2]
    dp_count = lax.axis_size(DP)
    fisher_sum = replica_squares(norm_rows, grad_rows, lengths[0])
    owned = sum_by_axis(fisher_sum, DP, 0)
    fisher = owned / (row_count * dp_count)
    return fisher[None]


def solution(mesh):
    split = Mesh(mesh.devices.reshape(mesh.shape["section"], 4, 8), ("section", "dp_0", "dp_1"))
    return jax.shard_map(
        per_device,
        mesh=split,
        in_specs=(
            P(DP, None),
            P(DP, None),
            P("section", DP, None),
            P("section", DP, None),
            P("section", None),
            P(DP, None),
        ),
        out_specs=P("section", DP, None),
        check_vma=False,
    )
```

profile of v0, /device:TPU:32, one launch (start us, length us, event | category | flops | bytes accessed | tf_op | source)
XLA Modules:
  0.0 725.6 jit_solution(15354992560067809190)
XLA Ops:
  16.0 92.8 %all-gather.2.cloned.1.call-done = bf16[2,8192,256]{2,1,0:T(8,128)(2,1)} async-done(((bf16[2,256,256]{2,1,0:T(8,128)(2,1)}), bf16[2,8192,256]{2,1,0:T(8,128)(2,1)}) %all-gather.2.cloned.1.call-update) | async-done | bytes 8388624 | tf_op jit(solution)/shard_map/all_gather | solution.py:20
  108.8 5.7 slice_bitcast_fusion
  115.2 183.5 %while.38 = (s32[]{:T(128)}, bf16[16,8192]{1,0:T(8,128)(2,1)S(1)}, bf16[128,8192]{1,0:T(8,128)(2,1)S(1)}, s32[]{:T(128)}, pred[]{:T(512)}, /*index=5*/bf16[128,8...) while((s32[]{:T(128)}, bf16[16,8192]{1,0:T(8,128)(2,1)S(1)}, ...), condition=%wide.region_4.5_spmd, body=%wide.region_0.4_spmd.sunk | while | flops 135680016 | bytes 11305566 | solution.py:118
  115.2 7.6 %conditional.4 = (bf16[16,8192]{1,0:T(8,128)(2,1)S(1)}, bf16[128,8192]{1,0:T(8,128)(2,1)S(1)}) conditional(s32[]{:T(128)} %convert_element_type.121, bf16[128,8192]{1,0:T(8,128)(2,1)S(1)} %get-tuple-element.844, (pred[]{:T(512)}, s32[]{:T(128)}, bf16[128,8192]{1,0:T(8,128)(2,1)}, bf16[16,8192]{1,0:T(8,128)(2,1)S(1)}, f32[1,8192]{1,0:T(1,128)S(1)}, ...), branch_computations={%region_1.1_spmd, %region_2.3_spmd} | conditional | flops 135680016 | bytes 10256731 | solution.py:109
  116.4 6.4 fusion
  125.3 7.6 %conditional.4 = (bf16[16,8192]{1,0:T(8,128)(2,1)S(1)}, bf16[128,8192]{1,0:T(8,128)(2,1)S(1)}) conditional(s32[]{:T(128)} %convert_element_type.121, bf16[128,8192]{1,0:T(8,128)(2,1)S(1)} %get-tuple-element.844, (pred[]{:T(512)}, s32[]{:T(128)}, bf16[128,8192]{1,0:T(8,128)(2,1)}, bf16[16,8192]{1,0:T(8,128)(2,1)S(1)}, f32[1,8192]{1,0:T(1,128)S(1)}, ...), branch_computations={%region_1.1_spmd, %region_2.3_spmd} | conditional | flops 135680016 | bytes 10256731 | solution.py:109
  126.5 6.4 fusion
  136.3 7.6 %conditional.4 = (bf16[16,8192]{1,0:T(8,128)(2,1)S(1)}, bf16[128,8192]{1,0:T(8,128)(2,1)S(1)}) conditional(s32[]{:T(128)} %convert_element_type.121, bf16[128,8192]{1,0:T(8,128)(2,1)S(1)} %get-tuple-element.844, (pred[]{:T(512)}, s32[]{:T(128)}, bf16[128,8192]{1,0:T(8,128)(2,1)}, bf16[16,8192]{1,0:T(8,128)(2,1)S(1)}, f32[1,8192]{1,0:T(1,128)S(1)}, ...), branch_computations={%region_1.1_spmd, %region_2.3_spmd} | conditional | flops 135680016 | bytes 10256731 | solution.py:109
  137.5 6.4 fusion
  143.9 4.1 collective-permute-start
  149.2 7.6 %conditional.4 = (bf16[16,8192]{1,0:T(8,128)(2,1)S(1)}, bf16[128,8192]{1,0:T(8,128)(2,1)S(1)}) conditional(s32[]{:T(128)} %convert_element_type.121, bf16[128,8192]{1,0:T(8,128)(2,1)S(1)} %get-tuple-element.844, (pred[]{:T(512)}, s32[]{:T(128)}, bf16[128,8192]{1,0:T(8,128)(2,1)}, bf16[16,8192]{1,0:T(8,128)(2,1)S(1)}, f32[1,8192]{1,0:T(1,128)S(1)}, ...), branch_computations={%region_1.1_spmd, %region_2.3_spmd} | conditional | flops 135680016 | bytes 10256731 | solution.py:109
  150.4 6.4 fusion
  156.8 6.6 collective-permute-start
  164.5 7.6 %conditional.4 = (bf16[16,8192]{1,0:T(8,128)(2,1)S(1)}, bf16[128,8192]{1,0:T(8,128)(2,1)S(1)}) conditional(s32[]{:T(128)} %convert_element_type.121, bf16[128,8192]{1,0:T(8,128)(2,1)S(1)} %get-tuple-element.844, (pred[]{:T(512)}, s32[]{:T(128)}, bf16[128,8192]{1,0:T(8,128)(2,1)}, bf16[16,8192]{1,0:T(8,128)(2,1)S(1)}, f32[1,8192]{1,0:T(1,128)S(1)}, ...), branch_computations={%region_1.1_spmd, %region_2.3_spmd} | conditional | flops 135680016 | bytes 10256731 | solution.py:109
  165.7 6.4 fusion
  172.1 6.6 collective-permute-start
  179.8 7.6 %conditional.4 = (bf16[16,8192]{1,0:T(8,128)(2,1)S(1)}, bf16[128,8192]{1,0:T(8,128)(2,1)S(1)}) conditional(s32[]{:T(128)} %convert_element_type.121, bf16[128,8192]{1,0:T(8,128)(2,1)S(1)} %get-tuple-element.844, (pred[]{:T(512)}, s32[]{:T(128)}, bf16[128,8192]{1,0:T(8,128)(2,1)}, bf16[16,8192]{1,0:T(8,128)(2,1)S(1)}, f32[1,8192]{1,0:T(1,128)S(1)}, ...), branch_computations={%region_1.1_spmd, %region_2.3_spmd} | conditional | flops 135680016 | bytes 10256731 | solution.py:109
  181.0 6.4 fusion
  187.4 6.6 collective-permute-start
  195.1 7.6 %conditional.4 = (bf16[16,8192]{1,0:T(8,128)(2,1)S(1)}, bf16[128,8192]{1,0:T(8,128)(2,1)S(1)}) conditional(s32[]{:T(128)} %convert_element_type.121, bf16[128,8192]{1,0:T(8,128)(2,1)S(1)} %get-tuple-element.844, (pred[]{:T(512)}, s32[]{:T(128)}, bf16[128,8192]{1,0:T(8,128)(2,1)}, bf16[16,8192]{1,0:T(8,128)(2,1)S(1)}, f32[1,8192]{1,0:T(1,128)S(1)}, ...), branch_computations={%region_1.1_spmd, %region_2.3_spmd} | conditional | flops 135680016 | bytes 10256731 | solution.py:109
  196.3 6.4 fusion
  202.7 6.6 collective-permute-start
  210.4 7.6 %conditional.4 = (bf16[16,8192]{1,0:T(8,128)(2,1)S(1)}, bf16[128,8192]{1,0:T(8,128)(2,1)S(1)}) conditional(s32[]{:T(128)} %convert_element_type.121, bf16[128,8192]{1,0:T(8,128)(2,1)S(1)} %get-tuple-element.844, (pred[]{:T(512)}, s32[]{:T(128)}, bf16[128,8192]{1,0:T(8,128)(2,1)}, bf16[16,8192]{1,0:T(8,128)(2,1)S(1)}, f32[1,8192]{1,0:T(1,128)S(1)}, ...), branch_computations={%region_1.1_spmd, %region_2.3_spmd} | conditional | flops 135680016 | bytes 10256731 | solution.py:109
  211.6 6.4 fusion
  218.0 6.6 collective-permute-start
  225.7 14.1 %collective-permute-start = (bf16[16,8192]{1,0:T(8,128)(2,1)S(1)}, bf16[16,8192]{1,0:T(8,128)(2,1)S(1)}, u32[]{:S(2)}, u32[]{:S(2)}) collective-permute-start(bf16[16,8192]{1,0:T(8,128)(2,1)S(1)} %get-tuple-element.804), channel_id=1, source_target_pairs={{0,32},{32,64},{64,96},{96,128},{128,160},{160,192},{192,224},{1,3... | collective-permute-start | bytes 786440 | tf_op jit(solution)/shard_map/while/body/eval_jaxpr/ppermute | solution.py:26
  241.0 6.6 collective-permute-start
  248.7 14.1 %collective-permute-start = (bf16[16,8192]{1,0:T(8,128)(2,1)S(1)}, bf16[16,8192]{1,0:T(8,128)(2,1)S(1)}, u32[]{:S(2)}, u32[]{:S(2)}) collective-permute-start(bf16[16,8192]{1,0:T(8,128)(2,1)S(1)} %get-tuple-element.804), channel_id=1, source_target_pairs={{0,32},{32,64},{64,96},{96,128},{128,160},{160,192},{192,224},{1,3... | collective-permute-start | bytes 786440 | tf_op jit(solution)/shard_map/while/body/eval_jaxpr/ppermute | solution.py:26
  264.0 6.6 collective-permute-start
  271.8 6.6 collective-permute-start
  279.5 6.6 collective-permute-start
  287.2 10.3 %collective-permute-start = (bf16[16,8192]{1,0:T(8,128)(2,1)S(1)}, bf16[16,8192]{1,0:T(8,128)(2,1)S(1)}, u32[]{:S(2)}, u32[]{:S(2)}) collective-permute-start(bf16[16,8192]{1,0:T(8,128)(2,1)S(1)} %get-tuple-element.804), channel_id=1, source_target_pairs={{0,32},{32,64},{64,96},{96,128},{128,160},{160,192},{192,224},{1,3... | collective-permute-start | bytes 786440 | tf_op jit(solution)/shard_map/while/body/eval_jaxpr/ppermute | solution.py:26
  300.3 284.3 %while.39 = (s32[]{:T(128)}, bf16[16,8192]{1,0:T(8,128)(2,1)S(1)}, bf16[128,8192]{1,0:T(8,128)(2,1)S(1)}, bf16[128,256]{1,0:T(8,128)(2,1)S(1)}, s32[]{:T(128)}, ...) while((s32[]{:T(128)}, bf16[16,8192]{1,0:T(8,128)(2,1)S(1)}, ...), condition=%wide.region_10.11_spmd, body=%wide.region_5.10_spmd.sunk | while | flops 204771360 | bytes 51276832 | solution.py:150
  301.7 6.3 collective-permute-done.1
  309.3 7.1 collective-permute-done.1
  317.7 6.4 collective-permute-done.1
  325.5 10.8 %collective-permute-done.1 = bf16[16,8192]{1,0:T(8,128)(2,1)S(1)} collective-permute-done((bf16[16,8192]{1,0:T(8,128)(2,1)S(1)}, bf16[16,8192]{1,0:T(8,128)(2,1)S(1)}, u32[]{:S(2)}, u32[]{:S(2)}) %collective-permute-start.1) | collective-permute-done | bytes 262176 | tf_op jit(solution)/shard_map/while/body/eval_jaxpr/ppermute | solution.py:26
  337.6 6.4 collective-permute-done.1
  345.4 7.0 collective-permute-done.1
  353.7 80.9 %collective-permute-done.1 = bf16[16,8192]{1,0:T(8,128)(2,1)S(1)} collective-permute-done((bf16[16,8192]{1,0:T(8,128)(2,1)S(1)}, bf16[16,8192]{1,0:T(8,128)(2,1)S(1)}, u32[]{:S(2)}, u32[]{:S(2)}) %collective-permute-start.1) | collective-permute-done | bytes 262176 | tf_op jit(solution)/shard_map/while/body/eval_jaxpr/ppermute | solution.py:26
  434.6 11.6 %conditional.5 = (bf16[16,8192]{1,0:T(8,128)(2,1)S(1)}, bf16[128,8192]{1,0:T(8,128)(2,1)S(1)}, bf16[128,256]{1,0:T(8,128)(2,1)S(1)}) conditional(s32[]{:T(128)} %convert_element_type.122, (bf16[128,8192]{1,0:T(8,128)(2,1)S(1)}, bf16[128,256]{1,0:T(8,128)(2,1)S(1)}) %tuple.120, (pred[]{:T(512)}, s32[]{:T(128)}, bf16[128,8192]{1,0:T(8,128)(2,1)}, ...), branch_computations={%region_6.6_spmd, %region_7.9_spmd} | conditional | flops 204771360 | bytes 50227948 | solution.py:140
  435.8 3.1 fusion.27
  447.5 6.4 collective-permute-done.1
  453.9 11.6 %conditional.5 = (bf16[16,8192]{1,0:T(8,128)(2,1)S(1)}, bf16[128,8192]{1,0:T(8,128)(2,1)S(1)}, bf16[128,256]{1,0:T(8,128)(2,1)S(1)}) conditional(s32[]{:T(128)} %convert_element_type.122, (bf16[128,8192]{1,0:T(8,128)(2,1)S(1)}, bf16[128,256]{1,0:T(8,128)(2,1)S(1)}) %tuple.120, (pred[]{:T(512)}, s32[]{:T(128)}, bf16[128,8192]{1,0:T(8,128)(2,1)}, ...), branch_computations={%region_6.6_spmd, %region_7.9_spmd} | conditional | flops 204771360 | bytes 50227948 | solution.py:140
  455.1 3.1 fusion.27
  466.8 6.4 collective-permute-done.1
  473.2 11.6 %conditional.5 = (bf16[16,8192]{1,0:T(8,128)(2,1)S(1)}, bf16[128,8192]{1,0:T(8,128)(2,1)S(1)}, bf16[128,256]{1,0:T(8,128)(2,1)S(1)}) conditional(s32[]{:T(128)} %convert_element_type.122, (bf16[128,8192]{1,0:T(8,128)(2,1)S(1)}, bf16[128,256]{1,0:T(8,128)(2,1)S(1)}) %tuple.120, (pred[]{:T(512)}, s32[]{:T(128)}, bf16[128,8192]{1,0:T(8,128)(2,1)}, ...), branch_computations={%region_6.6_spmd, %region_7.9_spmd} | conditional | flops 204771360 | bytes 50227948 | solution.py:140
  474.3 3.1 fusion.27
  486.1 6.4 collective-permute-done.1
  492.5 11.6 %conditional.5 = (bf16[16,8192]{1,0:T(8,128)(2,1)S(1)}, bf16[128,8192]{1,0:T(8,128)(2,1)S(1)}, bf16[128,256]{1,0:T(8,128)(2,1)S(1)}) conditional(s32[]{:T(128)} %convert_element_type.122, (bf16[128,8192]{1,0:T(8,128)(2,1)S(1)}, bf16[128,256]{1,0:T(8,128)(2,1)S(1)}) %tuple.120, (pred[]{:T(512)}, s32[]{:T(128)}, bf16[128,8192]{1,0:T(8,128)(2,1)}, ...), branch_computations={%region_6.6_spmd, %region_7.9_spmd} | conditional | flops 204771360 | bytes 50227948 | solution.py:140
  493.6 3.1 fusion.27
  505.4 6.4 collective-permute-done.1
  511.7 11.6 %conditional.5 = (bf16[16,8192]{1,0:T(8,128)(2,1)S(1)}, bf16[128,8192]{1,0:T(8,128)(2,1)S(1)}, bf16[128,256]{1,0:T(8,128)(2,1)S(1)}) conditional(s32[]{:T(128)} %convert_element_type.122, (bf16[128,8192]{1,0:T(8,128)(2,1)S(1)}, bf16[128,256]{1,0:T(8,128)(2,1)S(1)}) %tuple.120, (pred[]{:T(512)}, s32[]{:T(128)}, bf16[128,8192]{1,0:T(8,128)(2,1)}, ...), branch_computations={%region_6.6_spmd, %region_7.9_spmd} | conditional | flops 204771360 | bytes 50227948 | solution.py:140
  512.9 3.1 fusion.27
  524.6 6.4 collective-permute-done.1
  531.0 11.6 %conditional.5 = (bf16[16,8192]{1,0:T(8,128)(2,1)S(1)}, bf16[128,8192]{1,0:T(8,128)(2,1)S(1)}, bf16[128,256]{1,0:T(8,128)(2,1)S(1)}) conditional(s32[]{:T(128)} %convert_element_type.122, (bf16[128,8192]{1,0:T(8,128)(2,1)S(1)}, bf16[128,256]{1,0:T(8,128)(2,1)S(1)}) %tuple.120, (pred[]{:T(512)}, s32[]{:T(128)}, bf16[128,8192]{1,0:T(8,128)(2,1)}, ...), branch_computations={%region_6.6_spmd, %region_7.9_spmd} | conditional | flops 204771360 | bytes 50227948 | solution.py:140
  532.2 3.1 fusion.27
  543.9 6.4 collective-permute-done.1
  550.3 11.6 %conditional.5 = (bf16[16,8192]{1,0:T(8,128)(2,1)S(1)}, bf16[128,8192]{1,0:T(8,128)(2,1)S(1)}, bf16[128,256]{1,0:T(8,128)(2,1)S(1)}) conditional(s32[]{:T(128)} %convert_element_type.122, (bf16[128,8192]{1,0:T(8,128)(2,1)S(1)}, bf16[128,256]{1,0:T(8,128)(2,1)S(1)}) %tuple.120, (pred[]{:T(512)}, s32[]{:T(128)}, bf16[128,8192]{1,0:T(8,128)(2,1)}, ...), branch_computations={%region_6.6_spmd, %region_7.9_spmd} | conditional | flops 204771360 | bytes 50227948 | solution.py:140
  563.2 6.4 collective-permute-done.1
  569.6 11.6 %conditional.5 = (bf16[16,8192]{1,0:T(8,128)(2,1)S(1)}, bf16[128,8192]{1,0:T(8,128)(2,1)S(1)}, bf16[128,256]{1,0:T(8,128)(2,1)S(1)}) conditional(s32[]{:T(128)} %convert_element_type.122, (bf16[128,8192]{1,0:T(8,128)(2,1)S(1)}, bf16[128,256]{1,0:T(8,128)(2,1)S(1)}) %tuple.120, (pred[]{:T(512)}, s32[]{:T(128)}, bf16[128,8192]{1,0:T(8,128)(2,1)}, ...), branch_computations={%region_6.6_spmd, %region_7.9_spmd} | conditional | flops 204771360 | bytes 50227948 | solution.py:140
  588.8 4.6 fusion.33
  593.5 79.4 %reduce-scatter.3.cloned.1.call-done = f32[2048,256]{1,0:T(8,128)} async-done(((f32[8192,256]{1,0:T(8,128)}), f32[2048,256]{1,0:T(8,128)}) %reduce-scatter.3.cloned.1.call-update) | async-done | bytes 2097168 | tf_op jit(solution)/shard_map/reduce_scatter | solution.py:31
  672.9 44.5 %reduce-scatter.5.cloned.1.call-done = f32[256,256]{1,0:T(8,128)} async-done(((f32[2048,256]{1,0:T(8,128)}), f32[256,256]{1,0:T(8,128)}) %reduce-scatter.5.cloned.1.call-update) | async-done | bytes 262160 | tf_op jit(solution)/shard_map/reduce_scatter | solution.py:31
  (203 shorter events, 143.7 us)
Async XLA Ops:
  6.5 102.2 %all-gather.2.cloned.1.call-start = ((), (), s32[]{:S(2)}) async-start(), calls=%async_computation.2 | async-start | bytes 8650752 | tf_op jit(solution)/shard_map/all_gather | solution.py:20
  8.3 664.6 %reduce-scatter.3.cloned.1.call-start = ((), (), s32[]{:S(2)}) async-start(), calls=%async_computation.3 | async-start | bytes 10485760 | tf_op jit(solution)/shard_map/reduce_scatter | solution.py:31
  114.5 0.8 copy-start.3
  122.8 2.5 collective-permute-start
  132.9 3.4 collective-permute-start
  143.9 5.2 collective-permute-start
  156.8 7.7 %collective-permute-start = (bf16[16,8192]{1,0:T(8,128)(2,1)S(1)}, bf16[16,8192]{1,0:T(8,128)(2,1)S(1)}, u32[]{:S(2)}, u32[]{:S(2)}) collective-permute-start(bf16[16,8192]{1,0:T(8,128)(2,1)S(1)} %get-tuple-element.804), channel_id=1, source_target_pairs={{0,32},{32,64},{64,96},{96,128},{128,160},{160,192},{192,224},{1,3... | collective-permute-start | bytes 786440 | tf_op jit(solution)/shard_map/while/body/eval_jaxpr/ppermute | solution.py:26
  172.1 7.7 %collective-permute-start = (bf16[16,8192]{1,0:T(8,128)(2,1)S(1)}, bf16[16,8192]{1,0:T(8,128)(2,1)S(1)}, u32[]{:S(2)}, u32[]{:S(2)}) collective-permute-start(bf16[16,8192]{1,0:T(8,128)(2,1)S(1)} %get-tuple-element.804), channel_id=1, source_target_pairs={{0,32},{32,64},{64,96},{96,128},{128,160},{160,192},{192,224},{1,3... | collective-permute-start | bytes 786440 | tf_op jit(solution)/shard_map/while/body/eval_jaxpr/ppermute | solution.py:26
  187.4 7.7 %collective-permute-start = (bf16[16,8192]{1,0:T(8,128)(2,1)S(1)}, bf16[16,8192]{1,0:T(8,128)(2,1)S(1)}, u32[]{:S(2)}, u32[]{:S(2)}) collective-permute-start(bf16[16,8192]{1,0:T(8,128)(2,1)S(1)} %get-tuple-element.804), channel_id=1, source_target_pairs={{0,32},{32,64},{64,96},{96,128},{128,160},{160,192},{192,224},{1,3... | collective-permute-start | bytes 786440 | tf_op jit(solution)/shard_map/while/body/eval_jaxpr/ppermute | solution.py:26
  202.7 7.7 %collective-permute-start = (bf16[16,8192]{1,0:T(8,128)(2,1)S(1)}, bf16[16,8192]{1,0:T(8,128)(2,1)S(1)}, u32[]{:S(2)}, u32[]{:S(2)}) collective-permute-start(bf16[16,8192]{1,0:T(8,128)(2,1)S(1)} %get-tuple-element.804), channel_id=1, source_target_pairs={{0,32},{32,64},{64,96},{96,128},{128,160},{160,192},{192,224},{1,3... | collective-permute-start | bytes 786440 | tf_op jit(solution)/shard_map/while/body/eval_jaxpr/ppermute | solution.py:26
  218.0 7.7 %collective-permute-start = (bf16[16,8192]{1,0:T(8,128)(2,1)S(1)}, bf16[16,8192]{1,0:T(8,128)(2,1)S(1)}, u32[]{:S(2)}, u32[]{:S(2)}) collective-permute-start(bf16[16,8192]{1,0:T(8,128)(2,1)S(1)} %get-tuple-element.804), channel_id=1, source_target_pairs={{0,32},{32,64},{64,96},{96,128},{128,160},{160,192},{192,224},{1,3... | collective-permute-start | bytes 786440 | tf_op jit(solution)/shard_map/while/body/eval_jaxpr/ppermute | solution.py:26
  225.7 15.3 %collective-permute-start = (bf16[16,8192]{1,0:T(8,128)(2,1)S(1)}, bf16[16,8192]{1,0:T(8,128)(2,1)S(1)}, u32[]{:S(2)}, u32[]{:S(2)}) collective-permute-start(bf16[16,8192]{1,0:T(8,128)(2,1)S(1)} %get-tuple-element.804), channel_id=1, source_target_pairs={{0,32},{32,64},{64,96},{96,128},{128,160},{160,192},{192,224},{1,3... | collective-permute-start | bytes 786440 | tf_op jit(solution)/shard_map/while/body/eval_jaxpr/ppermute | solution.py:26
  241.0 7.7 %collective-permute-start = (bf16[16,8192]{1,0:T(8,128)(2,1)S(1)}, bf16[16,8192]{1,0:T(8,128)(2,1)S(1)}, u32[]{:S(2)}, u32[]{:S(2)}) collective-permute-start(bf16[16,8192]{1,0:T(8,128)(2,1)S(1)} %get-tuple-element.804), channel_id=1, source_target_pairs={{0,32},{32,64},{64,96},{96,128},{128,160},{160,192},{192,224},{1,3... | collective-permute-start | bytes 786440 | tf_op jit(solution)/shard_map/while/body/eval_jaxpr/ppermute | solution.py:26
  248.7 15.3 %collective-permute-start = (bf16[16,8192]{1,0:T(8,128)(2,1)S(1)}, bf16[16,8192]{1,0:T(8,128)(2,1)S(1)}, u32[]{:S(2)}, u32[]{:S(2)}) collective-permute-start(bf16[16,8192]{1,0:T(8,128)(2,1)S(1)} %get-tuple-element.804), channel_id=1, source_target_pairs={{0,32},{32,64},{64,96},{96,128},{128,160},{160,192},{192,224},{1,3... | collective-permute-start | bytes 786440 | tf_op jit(solution)/shard_map/while/body/eval_jaxpr/ppermute | solution.py:26
  264.0 7.7 %collective-permute-start = (bf16[16,8192]{1,0:T(8,128)(2,1)S(1)}, bf16[16,8192]{1,0:T(8,128)(2,1)S(1)}, u32[]{:S(2)}, u32[]{:S(2)}) collective-permute-start(bf16[16,8192]{1,0:T(8,128)(2,1)S(1)} %get-tuple-element.804), channel_id=1, source_target_pairs={{0,32},{32,64},{64,96},{96,128},{128,160},{160,192},{192,224},{1,3... | collective-permute-start | bytes 786440 | tf_op jit(solution)/shard_map/while/body/eval_jaxpr/ppermute | solution.py:26
  271.8 7.7 %collective-permute-start = (bf16[16,8192]{1,0:T(8,128)(2,1)S(1)}, bf16[16,8192]{1,0:T(8,128)(2,1)S(1)}, u32[]{:S(2)}, u32[]{:S(2)}) collective-permute-start(bf16[16,8192]{1,0:T(8,128)(2,1)S(1)} %get-tuple-element.804), channel_id=1, source_target_pairs={{0,32},{32,64},{64,96},{96,128},{128,160},{160,192},{192,224},{1,3... | collective-permute-start | bytes 786440 | tf_op jit(solution)/shard_map/while/body/eval_jaxpr/ppermute | solution.py:26
  279.5 7.7 %collective-permute-start = (bf16[16,8192]{1,0:T(8,128)(2,1)S(1)}, bf16[16,8192]{1,0:T(8,128)(2,1)S(1)}, u32[]{:S(2)}, u32[]{:S(2)}) collective-permute-start(bf16[16,8192]{1,0:T(8,128)(2,1)S(1)} %get-tuple-element.804), channel_id=1, source_target_pairs={{0,32},{32,64},{64,96},{96,128},{128,160},{160,192},{192,224},{1,3... | collective-permute-start | bytes 786440 | tf_op jit(solution)/shard_map/while/body/eval_jaxpr/ppermute | solution.py:26
  287.2 11.5 %collective-permute-start = (bf16[16,8192]{1,0:T(8,128)(2,1)S(1)}, bf16[16,8192]{1,0:T(8,128)(2,1)S(1)}, u32[]{:S(2)}, u32[]{:S(2)}) collective-permute-start(bf16[16,8192]{1,0:T(8,128)(2,1)S(1)} %get-tuple-element.804), channel_id=1, source_target_pairs={{0,32},{32,64},{64,96},{96,128},{128,160},{160,192},{192,224},{1,3... | collective-permute-start | bytes 786440 | tf_op jit(solution)/shard_map/while/body/eval_jaxpr/ppermute | solution.py:26
  298.7 1.3 copy-start.2
  300.4 7.6 %collective-permute-start.1 = (bf16[16,8192]{1,0:T(8,128)(2,1)S(1)}, bf16[16,8192]{1,0:T(8,128)(2,1)S(1)}, u32[]{:S(2)}, u32[]{:S(2)}) collective-permute-start(bf16[16,8192]{1,0:T(8,128)(2,1)S(1)} %get-tuple-element.817), channel_id=1, source_target_pairs={{32,0},{64,32},{96,64},{128,96},{160,128},{192,160},{224,192},{33,... | collective-permute-start | bytes 786440 | tf_op jit(solution)/shard_map/while/body/eval_jaxpr/ppermute | solution.py:26
  308.0 8.4 %collective-permute-start.1 = (bf16[16,8192]{1,0:T(8,128)(2,1)S(1)}, bf16[16,8192]{1,0:T(8,128)(2,1)S(1)}, u32[]{:S(2)}, u32[]{:S(2)}) collective-permute-start(bf16[16,8192]{1,0:T(8,128)(2,1)S(1)} %get-tuple-element.817), channel_id=1, source_target_pairs={{32,0},{64,32},{96,64},{128,96},{160,128},{192,160},{224,192},{33,... | collective-permute-start | bytes 786440 | tf_op jit(solution)/shard_map/while/body/eval_jaxpr/ppermute | solution.py:26
  316.4 7.7 %collective-permute-start.1 = (bf16[16,8192]{1,0:T(8,128)(2,1)S(1)}, bf16[16,8192]{1,0:T(8,128)(2,1)S(1)}, u32[]{:S(2)}, u32[]{:S(2)}) collective-permute-start(bf16[16,8192]{1,0:T(8,128)(2,1)S(1)} %get-tuple-element.817), channel_id=1, source_target_pairs={{32,0},{64,32},{96,64},{128,96},{160,128},{192,160},{224,192},{33,... | collective-permute-start | bytes 786440 | tf_op jit(solution)/shard_map/while/body/eval_jaxpr/ppermute | solution.py:26
  324.2 12.1 %collective-permute-start.1 = (bf16[16,8192]{1,0:T(8,128)(2,1)S(1)}, bf16[16,8192]{1,0:T(8,128)(2,1)S(1)}, u32[]{:S(2)}, u32[]{:S(2)}) collective-permute-start(bf16[16,8192]{1,0:T(8,128)(2,1)S(1)} %get-tuple-element.817), channel_id=1, source_target_pairs={{32,0},{64,32},{96,64},{128,96},{160,128},{192,160},{224,192},{33,... | collective-permute-start | bytes 786440 | tf_op jit(solution)/shard_map/while/body/eval_jaxpr/ppermute | solution.py:26
  336.3 7.7 %collective-permute-start.1 = (bf16[16,8192]{1,0:T(8,128)(2,1)S(1)}, bf16[16,8192]{1,0:T(8,128)(2,1)S(1)}, u32[]{:S(2)}, u32[]{:S(2)}) collective-permute-start(bf16[16,8192]{1,0:T(8,128)(2,1)S(1)} %get-tuple-element.817), channel_id=1, source_target_pairs={{32,0},{64,32},{96,64},{128,96},{160,128},{192,160},{224,192},{33,... | collective-permute-start | bytes 786440 | tf_op jit(solution)/shard_map/while/body/eval_jaxpr/ppermute | solution.py:26
  344.1 8.3 %collective-permute-start.1 = (bf16[16,8192]{1,0:T(8,128)(2,1)S(1)}, bf16[16,8192]{1,0:T(8,128)(2,1)S(1)}, u32[]{:S(2)}, u32[]{:S(2)}) collective-permute-start(bf16[16,8192]{1,0:T(8,128)(2,1)S(1)} %get-tuple-element.817), channel_id=1, source_target_pairs={{32,0},{64,32},{96,64},{128,96},{160,128},{192,160},{224,192},{33,... | collective-permute-start | bytes 786440 | tf_op jit(solution)/shard_map/while/body/eval_jaxpr/ppermute | solution.py:26
  352.4 82.2 %collective-permute-start.1 = (bf16[16,8192]{1,0:T(8,128)(2,1)S(1)}, bf16[16,8192]{1,0:T(8,128)(2,1)S(1)}, u32[]{:S(2)}, u32[]{:S(2)}) collective-permute-start(bf16[16,8192]{1,0:T(8,128)(2,1)S(1)} %get-tuple-element.817), channel_id=1, source_target_pairs={{32,0},{64,32},{96,64},{128,96},{160,128},{192,160},{224,192},{33,... | collective-permute-start | bytes 786440 | tf_op jit(solution)/shard_map/while/body/eval_jaxpr/ppermute | solution.py:26
  435.8 3.5 copy-start.1
  439.3 2.3 copy-start
  446.2 7.7 %collective-permute-start.1 = (bf16[16,8192]{1,0:T(8,128)(2,1)S(1)}, bf16[16,8192]{1,0:T(8,128)(2,1)S(1)}, u32[]{:S(2)}, u32[]{:S(2)}) collective-permute-start(bf16[16,8192]{1,0:T(8,128)(2,1)S(1)} %get-tuple-element.817), channel_id=1, source_target_pairs={{32,0},{64,32},{96,64},{128,96},{160,128},{192,160},{224,192},{33,... | collective-permute-start | bytes 786440 | tf_op jit(solution)/shard_map/while/body/eval_jaxpr/ppermute | solution.py:26
  455.0 3.5 copy-start.1
  458.6 2.3 copy-start
  465.5 7.7 %collective-permute-start.1 = (bf16[16,8192]{1,0:T(8,128)(2,1)S(1)}, bf16[16,8192]{1,0:T(8,128)(2,1)S(1)}, u32[]{:S(2)}, u32[]{:S(2)}) collective-permute-start(bf16[16,8192]{1,0:T(8,128)(2,1)S(1)} %get-tuple-element.817), channel_id=1, source_target_pairs={{32,0},{64,32},{96,64},{128,96},{160,128},{192,160},{224,192},{33,... | collective-permute-start | bytes 786440 | tf_op jit(solution)/shard_map/while/body/eval_jaxpr/ppermute | solution.py:26
  474.3 3.5 copy-start.1
  477.9 2.3 copy-start
  484.8 7.7 %collective-permute-start.1 = (bf16[16,8192]{1,0:T(8,128)(2,1)S(1)}, bf16[16,8192]{1,0:T(8,128)(2,1)S(1)}, u32[]{:S(2)}, u32[]{:S(2)}) collective-permute-start(bf16[16,8192]{1,0:T(8,128)(2,1)S(1)} %get-tuple-element.817), channel_id=1, source_target_pairs={{32,0},{64,32},{96,64},{128,96},{160,128},{192,160},{224,192},{33,... | collective-permute-start | bytes 786440 | tf_op jit(solution)/shard_map/while/body/eval_jaxpr/ppermute | solution.py:26
  493.6 3.5 copy-start.1
  497.1 2.3 copy-start
  504.1 7.7 %collective-permute-start.1 = (bf16[16,8192]{1,0:T(8,128)(2,1)S(1)}, bf16[16,8192]{1,0:T(8,128)(2,1)S(1)}, u32[]{:S(2)}, u32[]{:S(2)}) collective-permute-start(bf16[16,8192]{1,0:T(8,128)(2,1)S(1)} %get-tuple-element.817), channel_id=1, source_target_pairs={{32,0},{64,32},{96,64},{128,96},{160,128},{192,160},{224,192},{33,... | collective-permute-start | bytes 786440 | tf_op jit(solution)/shard_map/while/body/eval_jaxpr/ppermute | solution.py:26
  512.9 3.5 copy-start.1
  516.4 2.3 copy-start
  523.3 7.7 %collective-permute-start.1 = (bf16[16,8192]{1,0:T(8,128)(2,1)S(1)}, bf16[16,8192]{1,0:T(8,128)(2,1)S(1)}, u32[]{:S(2)}, u32[]{:S(2)}) collective-permute-start(bf16[16,8192]{1,0:T(8,128)(2,1)S(1)} %get-tuple-element.817), channel_id=1, source_target_pairs={{32,0},{64,32},{96,64},{128,96},{160,128},{192,160},{224,192},{33,... | collective-permute-start | bytes 786440 | tf_op jit(solution)/shard_map/while/body/eval_jaxpr/ppermute | solution.py:26
  532.2 3.5 copy-start.1
  535.7 2.3 copy-start
  542.6 7.7 %collective-permute-start.1 = (bf16[16,8192]{1,0:T(8,128)(2,1)S(1)}, bf16[16,8192]{1,0:T(8,128)(2,1)S(1)}, u32[]{:S(2)}, u32[]{:S(2)}) collective-permute-start(bf16[16,8192]{1,0:T(8,128)(2,1)S(1)} %get-tuple-element.817), channel_id=1, source_target_pairs={{32,0},{64,32},{96,64},{128,96},{160,128},{192,160},{224,192},{33,... | collective-permute-start | bytes 786440 | tf_op jit(solution)/shard_map/while/body/eval_jaxpr/ppermute | solution.py:26
  551.4 3.5 copy-start.1
  555.0 2.3 copy-start
  561.9 7.7 %collective-permute-start.1 = (bf16[16,8192]{1,0:T(8,128)(2,1)S(1)}, bf16[16,8192]{1,0:T(8,128)(2,1)S(1)}, u32[]{:S(2)}, u32[]{:S(2)}) collective-permute-start(bf16[16,8192]{1,0:T(8,128)(2,1)S(1)} %get-tuple-element.817), channel_id=1, source_target_pairs={{32,0},{64,32},{96,64},{128,96},{160,128},{192,160},{224,192},{33,... | collective-permute-start | bytes 786440 | tf_op jit(solution)/shard_map/while/body/eval_jaxpr/ppermute | solution.py:26
  570.7 3.5 copy-start.1
  574.3 2.3 copy-start
  581.2 3.4 collective-permute-start.1
  593.4 124.0 %reduce-scatter.5.cloned.1.call-start = ((), (), s32[]{:S(2)}) async-start(), calls=%async_computation.4 | async-start | bytes 2359296 | tf_op jit(solution)/shard_map/reduce_scatter | solution.py:31
Sparse Core Ops, SparseCore 0:
  9.9 98.8 all-gather.1
  593.5 79.2 reduce-scatter.2
  675.4 41.9 reduce-scatter.4
where the time goes:
time: 729 us; the launch traced here: 726 us
  waiting for transfers between devices  405 us (56%)
  starting transfers between devices  125 us (17%)
  matrix products  117 us (16%)
  other arithmetic  47.3 us (6%)
  local copies, waits for them, and re-layouts  17 us (2%)
  between operations  13.2 us (2%)
    ppermute x30, waiting for transfers between devices, from_behind(): return lax.ppermute(array, axis, pairs)  189 us
    ppermute x30, starting transfers between devices, from_behind(): return lax.ppermute(array, axis, pairs)  125 us
    reduce_scatter x2, waiting for transfers between devices, sum_by_axis(): array = lax.psum_scatter(array, axis, scatter_dimension=dim, tiled=True)  124 us
    all_gather x1, waiting for transfers between devices, side_by_side(): lax.all_gather(both, axis, axis=dim, tiled=True)  92.8 us
    dot_general x8, matrix products, layer_forward(): lax.dot_general(activated, w_up, (((1,), (1,)), ((), ())), preferred_elem...  51.1 us
    dot_general x8, matrix products, layer_backward(): pre_act = jnp.dot(normed, w_down, preferred_element_type=jnp.float32)  24.9 us
    dot_general x8, matrix products, layer_backward(): lax.dot_general(pre_grad, w_down, (((1,), (1,)), ((), ())), preferred_ele...  18.1 us
  transfers between devices with their start and end apart: 33, of which 33 were waited for; matrix products, arithmetic and copies ran while one was open for 1% of the time, Pallas kernels for 0%

commit v1 on v0

v1 whole, which is shorter than its diff:
```python
import functools

import jax
import jax.numpy as jnp
from jax import lax
from jax.experimental import pallas as pl
from jax.experimental.pallas import tpu as pltpu
from jax.sharding import Mesh
from jax.sharding import PartitionSpec as P

MESH = pl.DeviceIdType.MESH
F32 = jnp.float32
BF16 = jnp.bfloat16
NX, NZ, NS = 4, 8, 8
B = 256
D = 8192
R = 256
TOK = 128
MB = 16
NM = TOK // MB
EPS = 1e-05
PHASES = 4

GATHER_CHANNELS = 76
RS_CHANNELS = 76


def half(d):
    return pl.ds(0, 128) if d > 0 else pl.ds(128, 128)


def kernel(
    tok, cot, dwn, upw, gain, lens, out,
    wd, wu, hbuf, hout, nbuf, gbuf, gout, prebuf, invbuf, pgbuf, masked, fsum,
    rb_s, rb_r, ra_s, ra_r, gb, ga, sb_s, sb_r, sa_s, sa_r,
    lsem, ssem, grecv, frecv, brecv, rrecv, psem,
):
    s = lax.axis_index("section")
    x = lax.axis_index("x")
    z = lax.axis_index("z")

    def xo(k):
        return lax.rem(x + k + NX, NX)

    def zo(k):
        return lax.rem(z + k + NZ, NZ)

    own = (
        pltpu.make_async_copy(dwn, wd.at[x, z], lsem.at[0]),
        pltpu.make_async_copy(upw, wu.at[x, z], lsem.at[1]),
    )
    for c in own:
        c.start()

    barrier = pltpu.get_barrier_semaphore()
    s_next, s_prev = lax.rem(s + 1, NS), lax.rem(s + NS - 1, NS)
    for where in (
        {"x": xo(1)}, {"x": xo(-1)}, {"z": zo(1)}, {"z": zo(-1)},
        {"section": s_next}, {"section": s_prev},
    ):
        pl.semaphore_signal(barrier, inc=1, device_id=where, device_id_type=MESH)
    pl.semaphore_wait(barrier, 6)

    for c in own:
        c.wait()

    first = pltpu.make_async_copy(tok, hbuf, lsem.at[2])
    last = pltpu.make_async_copy(cot, gbuf, lsem.at[3])

    @pl.when(s == 0)
    def _():
        first.start()

    @pl.when(s == NS - 1)
    def _():
        last.start()

    sent = []
    counter = [0]
    chan = {}

    def number(key):
        if key not in chan:
            chan[key] = counter[0]
            counter[0] += 1
        return chan[key]

    def hop(axis, d):
        return {"x": xo(d)} if axis == "x" else {"z": zo(d)}

    def g_send(key, block, axis, d):
        k = number(key)
        c = pltpu.make_async_remote_copy(
            src_ref=block, dst_ref=block, send_sem=ssem.at[k], recv_sem=grecv.at[k],
            device_id=hop(axis, d), device_id_type=MESH,
        )
        c.start()
        sent.append(c)

    def g_wait(key, block, axis, d):
        k = number(key)
        pltpu.make_async_remote_copy(
            src_ref=block, dst_ref=block, send_sem=ssem.at[k], recv_sem=grecv.at[k],
            device_id=hop(axis, d), device_id_type=MESH,
        ).wait_recv()

    XOFF = (0, -1, 1, 2)
    ZOFF = (0, -1, 1, -2, 2, -3, 3, 4)

    def send_dx():
        for d in (1, -1):
            g_send(("dX", d), wd.at[x, z], "x", d)

    def wait_dx():
        for d in (1, -1):
            g_wait(("dX", d), wd.at[xo(-d), z], "x", d)

    def send_dx2():
        for d in (1, -1):
            g_send(("dX2", d), wd.at[xo(-d), z, half(d)], "x", d)

    def wait_dx2():
        for d in (1, -1):
            g_wait(("dX2", d), wd.at[xo(2), z, half(d)], "x", d)

    def send_uz(j):
        for d in (1, -1):
            blk = wu.at[x, zo(-d * (j - 1))]
            g_send(("uZ", d, j), blk if j < 4 else blk.at[half(d)], "z", d)

    def wait_uz(j):
        for d in (1, -1):
            blk = wu.at[x, zo(-d * j)]
            g_wait(("uZ", d, j), blk if j < 4 else blk.at[half(d)], "z", d)

    def send_dz(j, c):
        for d in (1, -1):
            blk = wd.at[xo(XOFF[c]), zo(-d * (j - 1))]
            g_send(("dZ", d, j, c), blk if j < 4 else blk.at[half(d)], "z", d)

    def wait_dz(j, c):
        for d in (1, -1):
            blk = wd.at[xo(XOFF[c]), zo(-d * j)]
            g_wait(("dZ", d, j, c), blk if j < 4 else blk.at[half(d)], "z", d)

    def send_ux(q):
        for d in (1, -1):
            g_send(("uX", d, q), wu.at[x, zo(ZOFF[q])], "x", d)

    def wait_ux(q):
        for d in (1, -1):
            g_wait(("uX", d, q), wu.at[xo(-d), zo(ZOFF[q])], "x", d)

    def send_ux2(q):
        for d in (1, -1):
            g_send(("uX2", d, q), wu.at[xo(-d), zo(ZOFF[q]), half(d)], "x", d)

    def wait_ux2(q):
        for d in (1, -1):
            g_wait(("uX2", d, q), wu.at[xo(2), zo(ZOFF[q]), half(d)], "x", d)

    def relay_ux(q):
        wait_ux(q)
        send_ux2(q)

    def relay_dz(j, c):
        wait_dz(j, c)
        send_dz(j + 1, c)

    send_dx()
    send_uz(1)
    send_dz(1, 0)
    send_ux(0)
    wait_dx()
    send_dx2()
    send_dz(1, 1)
    send_dz(1, 2)
    wait_uz(1)
    send_uz(2)
    send_ux(1)
    send_ux(2)
    wait_dx2()
    send_dz(1, 3)
    relay_ux(0)
    relay_dz(1, 0)
    wait_uz(2)
    send_uz(3)
    send_ux(3)
    send_ux(4)
    relay_ux(1)
    relay_ux(2)
    relay_dz(1, 1)
    relay_dz(1, 2)
    wait_uz(3)
    send_uz(4)
    send_ux(5)
    send_ux(6)
    relay_dz(1, 3)
    relay_dz(2, 0)
    relay_ux(3)
    relay_ux(4)
    relay_dz(2, 1)
    relay_dz(2, 2)
    wait_uz(4)
    send_ux(7)
    relay_dz(2, 3)
    relay_ux(5)
    relay_ux(6)
    for c in range(4):
        relay_dz(3, c)
    relay_ux(7)
    for c in range(4):
        wait_dz(4, c)
    for q in range(8):
        wait_ux2(q)
    for c in sent:
        c.wait_send()
    sent.clear()

    @pl.when(s == 0)
    def _():
        first.wait()

    @pl.when(s == NS - 1)
    def _():
        last.wait()

    def f_copy(i):
        return pltpu.make_async_remote_copy(
            src_ref=hout.at[i], dst_ref=hbuf.at[i], send_sem=psem.at[0, i], recv_sem=frecv.at[i],
            device_id={"section": s_next}, device_id_type=MESH,
        )

    def b_copy(i):
        return pltpu.make_async_remote_copy(
            src_ref=gout.at[i], dst_ref=gbuf.at[i], send_sem=psem.at[1, i], recv_sem=brecv.at[i],
            device_id={"section": s_prev}, device_id_type=MESH,
        )

    def blk(r):
        return slice(r * B, (r + 1) * B)

    def forward(i, carry):
        @pl.when(s > 0)
        def _():
            f_copy(i).wait_recv()

        rows = pl.ds(pl.multiple_of(i * MB, MB), MB)
        squares = jnp.zeros((MB, B), F32)
        for r in range(NX * NZ):
            h = hbuf[i, :, blk(r)].astype(F32)
            squares = squares + h * h
        inv = lax.rsqrt(jnp.sum(squares, axis=-1, keepdims=True) * (1.0 / D) + EPS)
        acc = jnp.zeros((MB, R), F32)
        for r in range(NX * NZ):
            h = hbuf[i, :, blk(r)].astype(F32)
            n = (h * inv * gain[:, blk(r)]).astype(BF16)
            nbuf[rows, blk(r)] = n
            acc = acc + jnp.dot(n, wd[r // NZ, r % NZ], preferred_element_type=F32)
        prebuf[rows, :] = acc
        invbuf[rows, :] = jnp.broadcast_to(inv, (MB, 128))
        act = (acc * jax.nn.sigmoid(acc)).astype(BF16)

        @pl.when(s < NS - 1)
        def _():
            for r in range(NX * NZ):
                up = lax.dot_general(
                    act, wu[r // NZ, r % NZ], (((1,), (1,)), ((), ())), preferred_element_type=F32
                )
                hout[i, :, blk(r)] = (hbuf[i, :, blk(r)].astype(F32) + up).astype(BF16)
            f_copy(i).start()

        return carry

    if PHASES >= 2:
        lax.fori_loop(0, NM, forward, 0)

    def backward(i, carry):
        @pl.when(s < NS - 1)
        def _():
            b_copy(i).wait_recv()

        rows = pl.ds(pl.multiple_of(i * MB, MB), MB)
        acc = jnp.zeros((MB, R), F32)
        for r in range(NX * NZ):
            acc = acc + jnp.dot(
                gbuf[i, :, blk(r)], wu[r // NZ, r % NZ], preferred_element_type=F32
            )
        pre = prebuf[rows, :]
        sig = jax.nn.sigmoid(pre)
        pg = (acc * sig * (1.0 + pre * (1.0 - sig))).astype(BF16)
        pgbuf[rows, :] = pg

        @pl.when(s > 0)
        def _():
            inv = invbuf[rows, 0:1]
            inner = jnp.sum(pg.astype(F32) * pre, axis=-1, keepdims=True) * (1.0 / D)
            coef = inv * inv * inner
            for r in range(NX * NZ):
                q = lax.dot_general(
                    pg, wd[r // NZ, r % NZ], (((1,), (1,)), ((), ())), preferred_element_type=F32
                )
                g = gbuf[i, :, blk(r)].astype(F32) + (
                    inv * (q * gain[:, blk(r)]) - coef * hbuf[i, :, blk(r)].astype(F32)
                )
                gout[i, :, blk(r)] = g.astype(BF16)
            b_copy(i).start()

        return carry

    if PHASES >= 3:
        lax.fori_loop(0, NM, backward, 0)

    if PHASES >= 2:
        @pl.when(s < NS - 1)
        def _():
            @pl.loop(0, NM)
            def _(i):
                f_copy(i).wait_send()

    if PHASES >= 3:
        @pl.when(s > 0)
        def _():
            @pl.loop(0, NM)
            def _(i):
                b_copy(i).wait_send()

    if PHASES < 4:
        out[...] = jnp.zeros((1, B, R), F32)
        return

    pgt = pgbuf[...].astype(F32).T
    position = lax.broadcasted_iota(jnp.int32, (1, TOK), 1)
    start = jnp.int32(0)
    for j in range(4):
        end = start + lens[0, j]
        inside = (position >= start) & (position < end)
        masked[j * R : (j + 1) * R, :] = jnp.where(inside, pgt, 0.0).astype(BF16)
        start = end

    for a in range(NX):
        @pl.loop(0, NZ)
        def _(b, a=a):
            cols = pl.ds(pl.multiple_of((a * NZ + b) * B, B), B)
            p = jnp.dot(masked[...], nbuf[:, cols], preferred_element_type=F32)
            p = p * p
            fsum[a, b] = (p[0:R] + p[R : 2 * R]) + (p[2 * R : 3 * R] + p[3 * R : 4 * R])

    rcount = [0]
    rchan = {}

    def rnumber(key):
        if key not in rchan:
            rchan[key] = rcount[0]
            rcount[0] += 1
        return rchan[key]

    def r_copy(key, src, dst, axis, d):
        k = rnumber(key)
        return pltpu.make_async_remote_copy(
            src_ref=src, dst_ref=dst, send_sem=ssem.at[k], recv_sem=rrecv.at[k],
            device_id=hop(axis, d), device_id_type=MESH,
        )

    def go(c):
        c.start()
        sent.append(c)

    def side(d):
        return 0 if d > 0 else 1

    def part(d):
        return slice(0, 64) if d > 0 else slice(64, 128)

    HALF, FULL = pl.ds(0, 64), pl.ds(0, 128)

    def ring(key, axis, depth, mine, sbuf, rbuf, d, j):
        e = side(d)
        span = HALF if j == depth else FULL
        value = mine(j * d)
        if j == depth:
            sbuf[e, j - 1, 0:64] = value[part(d)].astype(BF16)
        else:
            if j == depth - 1:
                r_copy(key + (d, j + 1), sbuf.at[e, j, HALF], rbuf.at[e, j, HALF], axis, d).wait_recv()
                got = rbuf[e, j, 0:64].astype(F32)
                fresh = part(d).start
                keep = 64 - fresh
                sbuf[e, j - 1, fresh : fresh + 64] = (value[part(d)] + got).astype(BF16)
                sbuf[e, j - 1, keep : keep + 64] = value[keep : keep + 64].astype(BF16)
            else:
                r_copy(key + (d, j + 1), sbuf.at[e, j, FULL], rbuf.at[e, j, FULL], axis, d).wait_recv()
                sbuf[e, j - 1] = (value + rbuf[e, j].astype(F32)).astype(BF16)
        go(r_copy(key + (d, j), sbuf.at[e, j - 1, span], rbuf.at[e, j - 1, span], axis, d))

    def ring_end(key, axis, mine, sbuf, rbuf):
        value = mine(0)
        for d in (1, -1):
            e = side(d)
            r_copy(key + (d, 1), sbuf.at[e, 0, FULL], rbuf.at[e, 0, FULL], axis, d).wait_recv()
            value = value + rbuf[e, 0].astype(F32)
        return value

    def stage_a(q, d, j):
        ring(("A1", q), "x", 2, lambda k: fsum[xo(k), q, 0:128], ra_s.at[q], ra_r.at[q], d, j)

    def stage_b(c, d, j):
        ring(("B1", c), "z", 4, lambda k: fsum[c, zo(k), 128:256], rb_s.at[c], rb_r.at[c], d, j)

    for c in range(NX):
        for d in (1, -1):
            stage_b(c, d, 4)
    for q in range(NZ):
        for d in (1, -1):
            stage_a(q, d, 2)
    for c in range(NX):
        for d in (1, -1):
            stage_b(c, d, 3)
    for q in range(NZ):
        for d in (1, -1):
            stage_a(q, d, 1)
    for c in range(NX):
        for d in (1, -1):
            stage_b(c, d, 2)
    for c in range(NX):
        for d in (1, -1):
            stage_b(c, d, 1)
    for q in range(NZ):
        ga[q] = ring_end(("A1", q), "x", lambda k: fsum[xo(k), q, 0:128], ra_s.at[q], ra_r.at[q])

    def last_a(d, j):
        ring(("A2",), "z", 4, lambda k: ga[zo(k)], sa_s, sa_r, d, j)

    def last_b(d, j):
        ring(("B2",), "x", 2, lambda k: gb[xo(k)], sb_s, sb_r, d, j)

    for d in (1, -1):
        last_a(d, 4)
    for c in range(NX):
        gb[c] = ring_end(("B1", c), "z", lambda k: fsum[c, zo(k), 128:256], rb_s.at[c], rb_r.at[c])
    for d in (1, -1):
        last_b(d, 2)
    for d in (1, -1):
        last_a(d, 3)
    for d in (1, -1):
        last_b(d, 1)
    for j in (2, 1):
        for d in (1, -1):
            last_a(d, j)
    low = ring_end(("A2",), "z", lambda k: ga[zo(k)], sa_s, sa_r)
    high = ring_end(("B2",), "x", lambda k: gb[xo(k)], sb_s, sb_r)
    scale = 1.0 / (TOK * NX * NZ)
    out[0, :, 0:128] = low.T * scale
    out[0, :, 128:256] = high.T * scale
    for c in sent:
        c.wait_send()


def per_device(tokens, cotangent, down_weight, up_weight, norm_gain, lengths):
    hbm = pl.BlockSpec(memory_space=pl.ANY)
    vmem = pl.BlockSpec(memory_space=pltpu.VMEM)
    dma = pltpu.SemaphoreType.DMA
    return pl.pallas_call(
        kernel,
        out_shape=jax.ShapeDtypeStruct((1, B, R), F32),
        in_specs=[hbm, hbm, hbm, hbm, vmem, pl.BlockSpec(memory_space=pltpu.SMEM)],
        out_specs=vmem,
        scratch_shapes=[
            pltpu.VMEM((NX, NZ, B, R), BF16),
            pltpu.VMEM((NX, NZ, B, R), BF16),
            pltpu.VMEM((NM, MB, D), BF16),
            pltpu.VMEM((NM, MB, D), BF16),
            pltpu.VMEM((TOK, D), BF16),
            pltpu.VMEM((NM, MB, D), BF16),
            pltpu.VMEM((NM, MB, D), BF16),
            pltpu.VMEM((TOK, R), F32),
            pltpu.VMEM((TOK, 128), F32),
            pltpu.VMEM((TOK, R), BF16),
            pltpu.VMEM((4 * R, TOK), BF16),
            pltpu.VMEM((NX, NZ, R, B), F32),
            pltpu.VMEM((NX, 2, 4, 128, B), BF16),
            pltpu.VMEM((NX, 2, 4, 128, B), BF16),
            pltpu.VMEM((NZ, 2, 2, 128, B), BF16),
            pltpu.VMEM((NZ, 2, 2, 128, B), BF16),
            pltpu.VMEM((NX, 128, B), F32),
            pltpu.VMEM((NZ, 128, B), F32),
            pltpu.VMEM((2, 2, 128, B), BF16),
            pltpu.VMEM((2, 2, 128, B), BF16),
            pltpu.VMEM((2, 4, 128, B), BF16),
            pltpu.VMEM((2, 4, 128, B), BF16),
            dma((4,)),
            dma((GATHER_CHANNELS,)),
            dma((GATHER_CHANNELS,)),
            dma((NM,)),
            dma((NM,)),
            dma((RS_CHANNELS,)),
            dma((2, NM)),
        ],
        compiler_params=pltpu.CompilerParams(
            collective_id=0, has_side_effects=True, vmem_limit_bytes=62 * 1024 * 1024
        ),
    )(
        tokens.reshape(NM, MB, D),
        cotangent.reshape(NM, MB, D),
        down_weight[0],
        up_weight[0],
        norm_gain,
        lengths,
    )


def solution(mesh):
    split = Mesh(mesh.devices.reshape(NS, NX, NZ), ("section", "x", "z"))
    dp = ("x", "z")
    return jax.shard_map(
        per_device,
        mesh=split,
        in_specs=(
            P(dp, None),
            P(dp, None),
            P("section", dp, None),
            P("section", dp, None),
            P("section", None),
            P(dp, None),
        ),
        out_specs=P("section", dp, None),
        check_vma=False,
    )
```

time: 729 us -> 214 us (0.29)
  waiting for transfers between devices: 405 us -> 0 us
  Pallas kernels: 0 us -> 212 us
  starting transfers between devices: 125 us -> 0 us
  matrix products: 117 us -> 0 us
  other arithmetic: 47.3 us -> 0 us
  local copies, waits for them, and re-layouts: 17 us -> 1.67 us
  between operations: 13.2 us -> 0.01 us
    pallas_call x0 -> x1, Pallas kernels: none -> 212 us  [per_device(): pl.pallas_call(kernel, out_shape=jax.ShapeDtypeStruct((1, B, R), F32), in...]
    ppermute x30 -> x0, waiting for transfers between devices: 189 us -> none  [from_behind(): return lax.ppermute(array, axis, pairs)]
    ppermute x30 -> x0, starting transfers between devices: 125 us -> none  [from_behind(): return lax.ppermute(array, axis, pairs)]
    reduce_scatter x2 -> x0, waiting for transfers between devices: 124 us -> none  [sum_by_axis(): array = lax.psum_scatter(array, axis, scatter_dimension=dim, tiled=True)]
    dot_general x36 -> x0, matrix products: 117 us -> none  [the longest x8 51.1 us: layer_forward(): lax.dot_general(activated, w_up, (((1,), (1,)), ((), ())), preferred_elem...]
    all_gather x1 -> x0, waiting for transfers between devices: 92.8 us -> none  [side_by_side(): lax.all_gather(both, axis, axis=dim, tiled=True)]
    dynamic_update_slice x16 -> x0, other arithmetic: 16.8 us -> none  [the longest x8 8.7 us: backward_compute_tick(): lax.dynamic_update_slice_in_dim(operands[1], normed, begin_row, 0)]
    reduce_sum x16 -> x0, other arithmetic: 10.5 us -> none  [the longest x8 9.03 us: layer_backward(): jnp.mean(wide_rows * wide_rows, axis=-1, keepdims=True) + epsilon]
  transfers between devices with their start and end apart: 33 -> 0, of which waited for: 33 -> 0; matrix products, arithmetic and copies ran while one was open for 1% -> 0% of each run, Pallas kernels for 0% -> 0%
where the time goes in v1:
time: 214 us
  Pallas kernels  212 us (99%)
    pallas_call x1, Pallas kernels, per_device(): pl.pallas_call(kernel, out_shape=jax.ShapeDtypeStruct((1, B, R), F32), in...  212 us

profile of v1, /device:TPU:32, one launch (start us, length us, event | category | flops | bytes accessed | tf_op | source)
XLA Modules:
  0.0 213.6 jit_solution(9877789858384711605)
XLA Ops:
  0.0 211.9 %shard_map.64 = f32[1,256,256]{2,1,0:T(8,128)} custom-call(bf16[8,16,8192]{2,1,0:T(8,128)(2,1)} %bitcast.4, bf16[8,16,8192]{2,1,0:T(8,128)(2,1)} %bitcast.5, bf16[256,256]{1,0:T(8,128)(2,1)} %bitcast.6, bf16[256,256]{1,0:T(8,128)(2,1)} %bitcast.7, f32[1,8192]{1,0:T(1,128)} %gain.1, s32[1,4]{1,0:T(1,128)} %lens.1), custom_call_target="tpu_custom_call" | custom-call | tf_op jit(solution)/shard_map/pallas_call | solution.py:463
  211.9 1.7 copy.8

commit v2 on v1

--- a/solution.py
+++ b/solution.py
@@ -19,7 +19,6 @@
 MB = 16
 NM = TOK // MB
 EPS = 1e-05
-PHASES = 4
 
 GATHER_CHANNELS = 76
 RS_CHANNELS = 76
@@ -31,9 +30,9 @@
 
 def kernel(
     tok, cot, dwn, upw, gain, lens, out,
-    wd, wu, hbuf, hout, nbuf, gbuf, gout, prebuf, invbuf, pgbuf, masked, fsum,
+    wd, wu, hbuf, hout, nbuf, cbuf, ebuf, mat, msg, gacc, hup, csum, actbuf, prebuf, invbuf, pgbuf, masked, fsum,
     rb_s, rb_r, ra_s, ra_r, gb, ga, sb_s, sb_r, sa_s, sa_r,
-    lsem, ssem, grecv, frecv, brecv, rrecv, psem,
+    lsem, ssem, grecv, frecv, brecv, rrecv, psem, bsend, esend, erecv, zsend, zrecv, xsend, xrecv,
 ):
     s = lax.axis_index("section")
     x = lax.axis_index("x")
@@ -56,24 +55,27 @@
     s_next, s_prev = lax.rem(s + 1, NS), lax.rem(s + NS - 1, NS)
     for where in (
         {"x": xo(1)}, {"x": xo(-1)}, {"z": zo(1)}, {"z": zo(-1)},
-        {"section": s_next}, {"section": s_prev},
+        *({"section": lax.rem(s + k, NS)} for k in range(1, NS)),
     ):
         pl.semaphore_signal(barrier, inc=1, device_id=where, device_id_type=MESH)
-    pl.semaphore_wait(barrier, 6)
+    pl.semaphore_wait(barrier, 3 + NS)
 
     for c in own:
         c.wait()
 
     first = pltpu.make_async_copy(tok, hbuf, lsem.at[2])
-    last = pltpu.make_async_copy(cot, gbuf, lsem.at[3])
+    cotangent = pltpu.make_async_copy(cot, cbuf, lsem.at[3])
+    cotangent.start()
+
+    def clear(j, carry):
+        ebuf[j] = jnp.zeros((16, D), BF16)
+        return carry
+
+    lax.fori_loop(0, s + 1, clear, 0)
 
     @pl.when(s == 0)
     def _():
         first.start()
-
-    @pl.when(s == NS - 1)
-    def _():
-        last.start()
 
     sent = []
     counter = [0]
@@ -221,45 +223,175 @@
     def _():
         first.wait()
 
-    @pl.when(s == NS - 1)
-    def _():
-        last.wait()
+    LATE = 6
+    EARLY = 4
+
+    def blk(r):
+        return slice(r * B, (r + 1) * B)
+
+    replica = x * NZ + z
+
+    def e_copy(j, below):
+        return pltpu.make_async_remote_copy(
+            src_ref=ebuf.at[j], dst_ref=ebuf.at[j], send_sem=esend.at[below], recv_sem=erecv.at[j],
+            device_id={"section": below}, device_id_type=MESH,
+        )
+
+    @pl.when(s > 0)
+    def _():
+        pick = lax.broadcasted_iota(jnp.int32, (8, R), 1) == (
+            lax.broadcasted_iota(jnp.int32, (8, R), 0) + replica * 8
+        )
+        pick = jnp.where(pick, 1.0, 0.0).astype(BF16)
+        for r in range(NX * NZ):
+            rows_d = lax.dot_general(
+                pick, wd[r // NZ, r % NZ], (((1,), (1,)), ((), ())), preferred_element_type=F32
+            )
+            rows_u = lax.dot_general(
+                pick, wu[r // NZ, r % NZ], (((1,), (1,)), ((), ())), preferred_element_type=F32
+            )
+            ebuf[s, :, blk(r)] = jnp.concatenate([rows_d * gain[:, blk(r)], rows_u], axis=0).astype(BF16)
+
+        def offer(t, carry):
+            e_copy(s, s - 1 - t).start()
+            return carry
+
+        lax.fori_loop(0, s, offer, 0)
+
+    def z_copy(j, h, d, arriving):
+        k = zo(-d * h) if arriving else zo(-d * (h - 1))
+        e = 0 if d > 0 else 1
+        ref = mat.at[j, :, x, k] if h < 4 else mat.at[j, e, x, k]
+        return pltpu.make_async_remote_copy(
+            src_ref=ref, dst_ref=ref, send_sem=zsend.at[j, 2 * h - 2 + e], recv_sem=zrecv.at[j, 2 * h - 2 + e],
+            device_id={"z": zo(d)}, device_id_type=MESH,
+        )
+
+    def x_copy(j, h, d, arriving):
+        k = xo(-d * h) if arriving else xo(-d * (h - 1))
+        e = 0 if d > 0 else 1
+        ref = mat.at[j, :, k] if h < 2 else mat.at[j, e, k]
+        return pltpu.make_async_remote_copy(
+            src_ref=ref, dst_ref=ref, send_sem=xsend.at[j, 2 * h - 2 + e], recv_sem=xrecv.at[j, 2 * h - 2 + e],
+            device_id={"x": xo(d)}, device_id_type=MESH,
+        )
+
+    def above(body):
+        def step(t, carry):
+            body(s + 1 + t)
+            return carry
+
+        lax.fori_loop(0, NS - 1 - s, step, 0)
+
+    def exchange_begin():
+        above(lambda j: e_copy(j, s_prev).wait_recv())
+        acc = jnp.zeros((NS * 16, R), F32)
+        for r in range(NX * NZ):
+            rows_e = ebuf[:, :, blk(r)].reshape(NS * 16, B)
+            acc = acc + jnp.dot(rows_e, wu[r // NZ, r % NZ], preferred_element_type=F32)
+        for j in range(1, NS):
+            mat[j, 0, x, z] = acc[16 * j : 16 * j + 8].astype(BF16)
+            mat[j, 1, x, z] = acc[16 * j + 8 : 16 * j + 16].astype(BF16)
+
+        def begin(j):
+            for d in (1, -1):
+                z_copy(j, 1, d, False).start()
+
+        above(begin)
+
+    def along(h):
+        def on(j):
+            for d in (1, -1):
+                z_copy(j, h, d, True).wait_recv()
+            for d in (1, -1):
+                z_copy(j, h + 1, d, False).start()
+
+        above(on)
+
+    def turn():
+        def one(j):
+            for d in (1, -1):
+                z_copy(j, 4, d, True).wait_recv()
+            for d in (1, -1):
+                x_copy(j, 1, d, False).start()
+
+        above(one)
+
+    def across():
+        def one(j):
+            for d in (1, -1):
+                x_copy(j, 1, d, True).wait_recv()
+            for d in (1, -1):
+                x_copy(j, 2, d, False).start()
+
+        above(one)
+
+    def finish():
+        def one(j):
+            for d in (1, -1):
+                x_copy(j, 2, d, True).wait_recv()
+
+        above(one)
+
+    exchange_steps = (
+        lambda: along(1), lambda: along(2), lambda: along(3), turn, across, finish,
+    )
+
+    def exchange_sent():
+        def one(j):
+            for d in (1, -1):
+                for h in (1, 2, 3, 4):
+                    z_copy(j, h, d, False).wait_send()
+                for h in (1, 2):
+                    x_copy(j, h, d, False).wait_send()
+
+        above(one)
+
+    def start_gradient():
+        cotangent.wait()
+        acc = jnp.zeros((TOK, R), F32)
+        for r in range(NX * NZ):
+            acc = acc + jnp.dot(cbuf[:, blk(r)], wu[r // NZ, r % NZ], preferred_element_type=F32)
+        gacc[...] = acc
+
+    @pl.when(s >= LATE)
+    def _():
+        start_gradient()
+
+    @pl.when((s > EARLY) & (s < NS - 1))
+    def _():
+        exchange_begin()
+
+    def micro(i):
+        return pl.ds(pl.multiple_of(i * MB, MB), MB)
 
     def f_copy(i):
         return pltpu.make_async_remote_copy(
-            src_ref=hout.at[i], dst_ref=hbuf.at[i], send_sem=psem.at[0, i], recv_sem=frecv.at[i],
+            src_ref=hout.at[micro(i)], dst_ref=hbuf.at[micro(i)], send_sem=psem.at[i], recv_sem=frecv.at[i],
             device_id={"section": s_next}, device_id_type=MESH,
         )
-
-    def b_copy(i):
-        return pltpu.make_async_remote_copy(
-            src_ref=gout.at[i], dst_ref=gbuf.at[i], send_sem=psem.at[1, i], recv_sem=brecv.at[i],
-            device_id={"section": s_prev}, device_id_type=MESH,
-        )
-
-    def blk(r):
-        return slice(r * B, (r + 1) * B)
 
     def forward(i, carry):
         @pl.when(s > 0)
         def _():
             f_copy(i).wait_recv()
 
-        rows = pl.ds(pl.multiple_of(i * MB, MB), MB)
+        rows = micro(i)
         squares = jnp.zeros((MB, B), F32)
         for r in range(NX * NZ):
-            h = hbuf[i, :, blk(r)].astype(F32)
+            h = hbuf[rows, blk(r)].astype(F32)
             squares = squares + h * h
         inv = lax.rsqrt(jnp.sum(squares, axis=-1, keepdims=True) * (1.0 / D) + EPS)
         acc = jnp.zeros((MB, R), F32)
         for r in range(NX * NZ):
-            h = hbuf[i, :, blk(r)].astype(F32)
+            h = hbuf[rows, blk(r)].astype(F32)
             n = (h * inv * gain[:, blk(r)]).astype(BF16)
             nbuf[rows, blk(r)] = n
             acc = acc + jnp.dot(n, wd[r // NZ, r % NZ], preferred_element_type=F32)
         prebuf[rows, :] = acc
         invbuf[rows, :] = jnp.broadcast_to(inv, (MB, 128))
         act = (acc * jax.nn.sigmoid(acc)).astype(BF16)
+        actbuf[rows, :] = act
 
         @pl.when(s < NS - 1)
         def _():
@@ -267,67 +399,83 @@
                 up = lax.dot_general(
                     act, wu[r // NZ, r % NZ], (((1,), (1,)), ((), ())), preferred_element_type=F32
                 )
-                hout[i, :, blk(r)] = (hbuf[i, :, blk(r)].astype(F32) + up).astype(BF16)
+                hout[rows, blk(r)] = (hbuf[rows, blk(r)].astype(F32) + up).astype(BF16)
             f_copy(i).start()
 
+        @pl.when((s >= EARLY) & (s < NS - 1))
+        def _():
+            @pl.when((s == EARLY) & (i == 1))
+            def _():
+                exchange_begin()
+
+            for k, step in enumerate(exchange_steps):
+                pl.when(i == jnp.where(s == EARLY, k + 2, k))(step)
+
         return carry
 
-    if PHASES >= 2:
-        lax.fori_loop(0, NM, forward, 0)
-
-    def backward(i, carry):
-        @pl.when(s < NS - 1)
-        def _():
-            b_copy(i).wait_recv()
-
-        rows = pl.ds(pl.multiple_of(i * MB, MB), MB)
-        acc = jnp.zeros((MB, R), F32)
+    lax.fori_loop(0, NM, forward, 0)
+
+    @pl.when(s < LATE)
+    def _():
+        start_gradient()
+
+    @pl.when(s < EARLY)
+    def _():
+        exchange_begin()
+        for step in exchange_steps:
+            step()
+
+    @pl.when(s < NS - 1)
+    def _():
+        acc = jnp.zeros((TOK, R), F32)
         for r in range(NX * NZ):
-            acc = acc + jnp.dot(
-                gbuf[i, :, blk(r)], wu[r // NZ, r % NZ], preferred_element_type=F32
-            )
-        pre = prebuf[rows, :]
-        sig = jax.nn.sigmoid(pre)
-        pg = (acc * sig * (1.0 + pre * (1.0 - sig))).astype(BF16)
-        pgbuf[rows, :] = pg
+            acc = acc + jnp.dot(hout[:, blk(r)], wu[r // NZ, r % NZ], preferred_element_type=F32)
+        hup[...] = acc
+
+    csum[...] = jnp.zeros((TOK, 128), F32)
+
+    def b_copy(j):
+        return pltpu.make_async_remote_copy(
+            src_ref=msg.at[j], dst_ref=msg.at[j], send_sem=bsend.at[j], recv_sem=brecv.at[j],
+            device_id={"section": s_prev}, device_id_type=MESH,
+        )
+
+    def arrive(t, carry):
+        j = NS - 1 - t
+        b_copy(j).wait_recv()
 
         @pl.when(s > 0)
         def _():
-            inv = invbuf[rows, 0:1]
-            inner = jnp.sum(pg.astype(F32) * pre, axis=-1, keepdims=True) * (1.0 / D)
-            coef = inv * inv * inner
-            for r in range(NX * NZ):
-                q = lax.dot_general(
-                    pg, wd[r // NZ, r % NZ], (((1,), (1,)), ((), ())), preferred_element_type=F32
-                )
-                g = gbuf[i, :, blk(r)].astype(F32) + (
-                    inv * (q * gain[:, blk(r)]) - coef * hbuf[i, :, blk(r)].astype(F32)
-                )
-                gout[i, :, blk(r)] = g.astype(BF16)
-            b_copy(i).start()
-
+            b_copy(j).start()
+
+        c = msg[j, :, 2 * R : 2 * R + 128].astype(F32)
+        csum[...] += c
+        from_down = jnp.dot(
+            msg[j, :, 0:R], mat[j, 0].reshape(R, R), preferred_element_type=F32
+        )
+        from_up = jnp.dot(
+            msg[j, :, R : 2 * R], mat[j, 1].reshape(R, R), preferred_element_type=F32
+        )
+        both = jnp.concatenate([c, c], axis=1)
+        gacc[...] += from_down + from_up - both * hup[...]
         return carry
 
-    if PHASES >= 3:
-        lax.fori_loop(0, NM, backward, 0)
-
-    if PHASES >= 2:
-        @pl.when(s < NS - 1)
-        def _():
-            @pl.loop(0, NM)
-            def _(i):
-                f_copy(i).wait_send()
-
-    if PHASES >= 3:
-        @pl.when(s > 0)
-        def _():
-            @pl.loop(0, NM)
-            def _(i):
-                b_copy(i).wait_send()
-
-    if PHASES < 4:
-        out[...] = jnp.zeros((1, B, R), F32)
-        return
+    lax.fori_loop(0, NS - 1 - s, arrive, 0)
+
+    pre = prebuf[...]
+    sig = jax.nn.sigmoid(pre)
+    pg = (gacc[...] * sig * (1.0 + pre * (1.0 - sig))).astype(BF16)
+    pgbuf[...] = pg
+
+    @pl.when(s > 0)
+    def _():
+        wide = pg.astype(F32)
+        inv = invbuf[:, 0:1]
+        coef = inv * inv * (jnp.sum(wide * pre, axis=-1, keepdims=True) * (1.0 / D))
+        msg[s, :, 0:R] = (wide * inv).astype(BF16)
+        msg[s, :, R : 2 * R] = (actbuf[...].astype(F32) * (-csum[:, 0:1])).astype(BF16)
+        msg[s, :, 2 * R : 2 * R + 128] = jnp.broadcast_to(coef, (TOK, 128)).astype(BF16)
+        b_copy(s).start()
 
     pgt = pgbuf[...].astype(F32).T
     position = lax.broadcasted_iota(jnp.int32, (1, TOK), 1)
@@ -455,6 +603,28 @@
     for c in sent:
         c.wait_send()
 
+    exchange_sent()
+
+    @pl.when(s < NS - 1)
+    def _():
+        @pl.loop(0, NM)
+        def _(i):
+            f_copy(i).wait_send()
+
+    @pl.when(s > 0)
+    def _():
+        def done(t, carry):
+            b_copy(s + t).wait_send()
+            return carry
+
+        lax.fori_loop(0, NS - s, done, 0)
+
+        def offered(t, carry):
+            e_copy(s, t).wait_send()
+            return carry
+
+        lax.fori_loop(0, s, offered, 0)
+
 
 def per_device(tokens, cotangent, down_weight, up_weight, norm_gain, lengths):
     hbm = pl.BlockSpec(memory_space=pl.ANY)
@@ -468,11 +638,17 @@
         scratch_shapes=[
             pltpu.VMEM((NX, NZ, B, R), BF16),
             pltpu.VMEM((NX, NZ, B, R), BF16),
-            pltpu.VMEM((NM, MB, D), BF16),
-            pltpu.VMEM((NM, MB, D), BF16),
             pltpu.VMEM((TOK, D), BF16),
-            pltpu.VMEM((NM, MB, D), BF16),
-            pltpu.VMEM((NM, MB, D), BF16),
+            pltpu.VMEM((TOK, D), BF16),
+            pltpu.VMEM((TOK, D), BF16),
+            pltpu.VMEM((TOK, D), BF16),
+            pltpu.VMEM((NS, 16, D), BF16),
+            pltpu.VMEM((NS, 2, NX, NZ, 8, R), BF16),
+            pltpu.VMEM((NS, TOK, 2 * R + 128), BF16),
+            pltpu.VMEM((TOK, R), F32),
+            pltpu.VMEM((TOK, R), F32),
+            pltpu.VMEM((TOK, 128), F32),
+            pltpu.VMEM((TOK, R), BF16),
             pltpu.VMEM((TOK, R), F32),
             pltpu.VMEM((TOK, 128), F32),
             pltpu.VMEM((TOK, R), BF16),
@@ -492,16 +668,23 @@
             dma((GATHER_CHANNELS,)),
             dma((GATHER_CHANNELS,)),
             dma((NM,)),
+            dma((NS,)),
+            dma((RS_CHANNELS,)),
             dma((NM,)),
-            dma((RS_CHANNELS,)),
-            dma((2, NM)),
+            dma((NS,)),
+            dma((NS,)),
+            dma((NS,)),
+            dma((NS, 8)),
+            dma((NS, 8)),
+            dma((NS, 4)),
+            dma((NS, 4)),
         ],
         compiler_params=pltpu.CompilerParams(
             collective_id=0, has_side_effects=True, vmem_limit_bytes=62 * 1024 * 1024
         ),
     )(
-        tokens.reshape(NM, MB, D),
-        cotangent.reshape(NM, MB, D),
+        tokens,
+        cotangent,
         down_weight[0],
         up_weight[0],
         norm_gain,

time: 214 us -> 194 us (0.907)
  Pallas kernels: 212 us -> 192 us
    pallas_call x1, Pallas kernels: 212 us -> 192 us  [per_device(): pl.pallas_call(kernel, out_shape=jax.ShapeDtypeStruct((1, B, R), F32), in...]
where the time goes in v2:
time: 194 us; the launch traced here: 193 us
  Pallas kernels  192 us (99%)
    pallas_call x1, Pallas kernels, per_device(): pl.pallas_call(kernel, out_shape=jax.ShapeDtypeStruct((1, B, R), F32), in...  192 us

profile of v2, /device:TPU:32, one launch (start us, length us, event | category | flops | bytes accessed | tf_op | source)
XLA Modules:
  0.0 193.4 jit_solution(3538421215085762333)
XLA Ops:
  0.0 191.7 %shard_map.64 = f32[1,256,256]{2,1,0:T(8,128)} custom-call(bf16[128,8192]{1,0:T(8,128)(2,1)} %tok.1, bf16[128,8192]{1,0:T(8,128)(2,1)} %cot.1, bf16[256,256]{1,0:T(8,128)(2,1)} %bitcast.2, bf16[256,256]{1,0:T(8,128)(2,1)} %bitcast.3, f32[1,8192]{1,0:T(1,128)} %gain.1, s32[1,4]{1,0:T(1,128)} %lens.1), custom_call_target="tpu_custom_call" | custom-call | tf_op jit(solution)/shard_map/pallas_call | solution.py:633
  191.7 1.7 copy.8

commit v3 on v2

--- a/solution.py
+++ b/solution.py
@@ -17,6 +17,9 @@
 R = 256
 TOK = 128
 MB = 16
+XROWS = 128
+NC = 4
+PER = NX * NZ // NC
 NM = TOK // MB
 EPS = 1e-05
 
@@ -24,15 +27,25 @@
 RS_CHANNELS = 76
 
 
-def half(d):
-    return pl.ds(0, 128) if d > 0 else pl.ds(128, 128)
+CUT = 304
+
+
+def half_z(d):
+    return pl.ds(0, 160) if d > 0 else pl.ds(160, CUT - 160)
+
+
+def half_x(d):
+    return pl.ds(CUT, 112) if d > 0 else pl.ds(CUT + 112, 96)
+
+
+ZFIRST, XFIRST = pl.ds(0, CUT), pl.ds(CUT, 2 * B - CUT)
 
 
 def kernel(
     tok, cot, dwn, upw, gain, lens, out,
-    wd, wu, hbuf, hout, nbuf, cbuf, ebuf, mat, msg, gacc, hup, csum, actbuf, prebuf, invbuf, pgbuf, masked, fsum,
+    w, hbuf, hout, nbuf, cbuf, ebuf, mat, msg, gacc, hup, csum, actbuf, prebuf, invbuf, pgbuf, masked, fsum,
     rb_s, rb_r, ra_s, ra_r, gb, ga, sb_s, sb_r, sa_s, sa_r,
-    lsem, ssem, grecv, frecv, brecv, rrecv, psem, bsend, esend, erecv, zsend, zrecv, xsend, xrecv,
+    lsem, ssem, grecv, frecv, brecv, rrecv, psem, bsend, esend, erecv, hsend, zsend, zrecv, xsend, xrecv,
 ):
     s = lax.axis_index("section")
     x = lax.axis_index("x")
@@ -45,8 +58,8 @@
         return lax.rem(z + k + NZ, NZ)
 
     own = (
-        pltpu.make_async_copy(dwn, wd.at[x, z], lsem.at[0]),
-        pltpu.make_async_copy(upw, wu.at[x, z], lsem.at[1]),
+        pltpu.make_async_copy(dwn, w.at[x, z, pl.ds(B, B)], lsem.at[0]),
+        pltpu.make_async_copy(upw, w.at[x, z, pl.ds(0, B)], lsem.at[1]),
     )
     for c in own:
         c.start()
@@ -111,55 +124,55 @@
 
     def send_dx():
         for d in (1, -1):
-            g_send(("dX", d), wd.at[x, z], "x", d)
+            g_send(("dX", d), w.at[x, z, XFIRST], "x", d)
 
     def wait_dx():
         for d in (1, -1):
-            g_wait(("dX", d), wd.at[xo(-d), z], "x", d)
+            g_wait(("dX", d), w.at[xo(-d), z, XFIRST], "x", d)
 
     def send_dx2():
         for d in (1, -1):
-            g_send(("dX2", d), wd.at[xo(-d), z, half(d)], "x", d)
+            g_send(("dX2", d), w.at[xo(-d), z, half_x(d)], "x", d)
 
     def wait_dx2():
         for d in (1, -1):
-            g_wait(("dX2", d), wd.at[xo(2), z, half(d)], "x", d)
+            g_wait(("dX2", d), w.at[xo(2), z, half_x(d)], "x", d)
 
     def send_uz(j):
         for d in (1, -1):
-            blk = wu.at[x, zo(-d * (j - 1))]
-            g_send(("uZ", d, j), blk if j < 4 else blk.at[half(d)], "z", d)
+            rows = ZFIRST if j < 4 else half_z(d)
+            g_send(("uZ", d, j), w.at[x, zo(-d * (j - 1)), rows], "z", d)
 
     def wait_uz(j):
         for d in (1, -1):
-            blk = wu.at[x, zo(-d * j)]
-            g_wait(("uZ", d, j), blk if j < 4 else blk.at[half(d)], "z", d)
+            rows = ZFIRST if j < 4 else half_z(d)
+            g_wait(("uZ", d, j), w.at[x, zo(-d * j), rows], "z", d)
 
     def send_dz(j, c):
         for d in (1, -1):
-            blk = wd.at[xo(XOFF[c]), zo(-d * (j - 1))]
-            g_send(("dZ", d, j, c), blk if j < 4 else blk.at[half(d)], "z", d)
+            rows = XFIRST if j < 4 else half_x(d)
+            g_send(("dZ", d, j, c), w.at[xo(XOFF[c]), zo(-d * (j - 1)), rows], "z", d)
 
     def wait_dz(j, c):
         for d in (1, -1):
-            blk = wd.at[xo(XOFF[c]), zo(-d * j)]
-            g_wait(("dZ", d, j, c), blk if j < 4 else blk.at[half(d)], "z", d)
+            rows = XFIRST if j < 4 else half_x(d)
+            g_wait(("dZ", d, j, c), w.at[xo(XOFF[c]), zo(-d * j), rows], "z", d)
 
     def send_ux(q):
         for d in (1, -1):
-            g_send(("uX", d, q), wu.at[x, zo(ZOFF[q])], "x", d)
+            g_send(("uX", d, q), w.at[x, zo(ZOFF[q]), ZFIRST], "x", d)
 
     def wait_ux(q):
         for d in (1, -1):
-            g_wait(("uX", d, q), wu.at[xo(-d), zo(ZOFF[q])], "x", d)
+            g_wait(("uX", d, q), w.at[xo(-d), zo(ZOFF[q]), ZFIRST], "x", d)
 
     def send_ux2(q):
         for d in (1, -1):
-            g_send(("uX2", d, q), wu.at[xo(-d), zo(ZOFF[q]), half(d)], "x", d)
+            g_send(("uX2", d, q), w.at[xo(-d), zo(ZOFF[q]), half_z(d)], "x", d)
 
     def wait_ux2(q):
         for d in (1, -1):
-            g_wait(("uX2", d, q), wu.at[xo(2), zo(ZOFF[q]), half(d)], "x", d)
+            g_wait(("uX2", d, q), w.at[xo(2), zo(ZOFF[q]), half_z(d)], "x", d)
 
     def relay_ux(q):
         wait_ux(q)
@@ -223,13 +236,15 @@
     def _():
         first.wait()
 
-    LATE = 6
-    EARLY = 4
+    LATE = 4
+    begin_at = jnp.where(s >= 5, -1, jnp.where(s == 4, 1, jnp.where(s == 3, 5, jnp.where(s == 2, 6, NM))))
+    hand_at = jnp.where(s >= 5, -1, jnp.where(s == 3, 4, NM - 1))
 
     def blk(r):
         return slice(r * B, (r + 1) * B)
 
     replica = x * NZ + z
+    odd = lax.rem(s, 2)
 
     def e_copy(j, below):
         return pltpu.make_async_remote_copy(
@@ -245,18 +260,22 @@
         pick = jnp.where(pick, 1.0, 0.0).astype(BF16)
         for r in range(NX * NZ):
             rows_d = lax.dot_general(
-                pick, wd[r // NZ, r % NZ], (((1,), (1,)), ((), ())), preferred_element_type=F32
+                pick, w[r // NZ, r % NZ, B : 2 * B], (((1,), (1,)), ((), ())), preferred_element_type=F32
             )
             rows_u = lax.dot_general(
-                pick, wu[r // NZ, r % NZ], (((1,), (1,)), ((), ())), preferred_element_type=F32
+                pick, w[r // NZ, r % NZ, 0:B], (((1,), (1,)), ((), ())), preferred_element_type=F32
             )
             ebuf[s, :, blk(r)] = jnp.concatenate([rows_d * gain[:, blk(r)], rows_u], axis=0).astype(BF16)
 
+        @pl.when(odd == 1)
+        def _():
+            e_copy(s, s - 1).start()
+
         def offer(t, carry):
-            e_copy(s, s - 1 - t).start()
+            e_copy(s, s - 1 - odd - 2 * t).start()
             return carry
 
-        lax.fori_loop(0, s, offer, 0)
+        lax.fori_loop(0, s // 2, offer, 0)
 
     def z_copy(j, h, d, arriving):
         k = zo(-d * h) if arriving else zo(-d * (h - 1))
@@ -283,12 +302,31 @@
 
         lax.fori_loop(0, NS - 1 - s, step, 0)
 
+    def hand_on():
+        def one(j):
+            e_copy(j, s_prev).wait_recv()
+            pltpu.make_async_remote_copy(
+                src_ref=ebuf.at[j], dst_ref=ebuf.at[j], send_sem=hsend.at[j], recv_sem=erecv.at[j],
+                device_id={"section": s_prev}, device_id_type=MESH,
+            ).start()
+
+        above(one)
+
+    def handed():
+        above(lambda j: pltpu.make_async_remote_copy(
+            src_ref=ebuf.at[j], dst_ref=ebuf.at[j], send_sem=hsend.at[j], recv_sem=erecv.at[j],
+            device_id={"section": s_prev}, device_id_type=MESH,
+        ).wait_send())
+
     def exchange_begin():
-        above(lambda j: e_copy(j, s_prev).wait_recv())
+        @pl.when(odd == 0)
+        def _():
+            above(lambda j: e_copy(j, s_prev).wait_recv())
+
         acc = jnp.zeros((NS * 16, R), F32)
         for r in range(NX * NZ):
             rows_e = ebuf[:, :, blk(r)].reshape(NS * 16, B)
-            acc = acc + jnp.dot(rows_e, wu[r // NZ, r % NZ], preferred_element_type=F32)
+            acc = acc + jnp.dot(rows_e, w[r // NZ, r % NZ, 0:B], preferred_element_type=F32)
         for j in range(1, NS):
             mat[j, 0, x, z] = acc[16 * j : 16 * j + 8].astype(BF16)
             mat[j, 1, x, z] = acc[16 * j + 8 : 16 * j + 16].astype(BF16)
@@ -351,43 +389,51 @@
         cotangent.wait()
         acc = jnp.zeros((TOK, R), F32)
         for r in range(NX * NZ):
-            acc = acc + jnp.dot(cbuf[:, blk(r)], wu[r // NZ, r % NZ], preferred_element_type=F32)
+            acc = acc + jnp.dot(cbuf[:, blk(r)], w[r // NZ, r % NZ, 0:B], preferred_element_type=F32)
         gacc[...] = acc
 
     @pl.when(s >= LATE)
     def _():
         start_gradient()
 
-    @pl.when((s > EARLY) & (s < NS - 1))
+    @pl.when((odd == 1) & (hand_at < 0))
+    def _():
+        hand_on()
+
+    @pl.when((begin_at < 0) & (s < NS - 1))
     def _():
         exchange_begin()
 
     def micro(i):
         return pl.ds(pl.multiple_of(i * MB, MB), MB)
 
-    def f_copy(i):
+    def f_copy(i, q):
+        cols = pl.ds(q * PER * B, PER * B)
         return pltpu.make_async_remote_copy(
-            src_ref=hout.at[micro(i)], dst_ref=hbuf.at[micro(i)], send_sem=psem.at[i], recv_sem=frecv.at[i],
+            src_ref=hout.at[micro(i), cols], dst_ref=hbuf.at[micro(i), cols],
+            send_sem=psem.at[i, q], recv_sem=frecv.at[i, q],
             device_id={"section": s_next}, device_id_type=MESH,
         )
 
     def forward(i, carry):
-        @pl.when(s > 0)
-        def _():
-            f_copy(i).wait_recv()
-
         rows = micro(i)
         squares = jnp.zeros((MB, B), F32)
-        for r in range(NX * NZ):
-            h = hbuf[rows, blk(r)].astype(F32)
-            squares = squares + h * h
+        accs = [jnp.zeros((MB, 128), F32)] * 2
+        for q in range(NC):
+            @pl.when(s > 0)
+            def _(q=q):
+                f_copy(i, q).wait_recv()
+
+            for r in range(q * PER, (q + 1) * PER):
+                h = hbuf[rows, blk(r)].astype(F32)
+                squares = squares + h * h
+                n = (h * gain[:, blk(r)]).astype(BF16)
+                nbuf[rows, blk(r)] = n
+                for e in range(2):
+                    cut = w[r // NZ, r % NZ, B : 2 * B, e * 128 : (e + 1) * 128]
+                    accs[e] = accs[e] + jnp.dot(n, cut, preferred_element_type=F32)
         inv = lax.rsqrt(jnp.sum(squares, axis=-1, keepdims=True) * (1.0 / D) + EPS)
-        acc = jnp.zeros((MB, R), F32)
-        for r in range(NX * NZ):
-            h = hbuf[rows, blk(r)].astype(F32)
-            n = (h * inv * gain[:, blk(r)]).astype(BF16)
-            nbuf[rows, blk(r)] = n
-            acc = acc + jnp.dot(n, wd[r // NZ, r % NZ], preferred_element_type=F32)
+        acc = jnp.concatenate(accs, axis=1) * inv
         prebuf[rows, :] = acc
         invbuf[rows, :] = jnp.broadcast_to(inv, (MB, 128))
         act = (acc * jax.nn.sigmoid(acc)).astype(BF16)
@@ -395,87 +441,106 @@
 
         @pl.when(s < NS - 1)
         def _():
-            for r in range(NX * NZ):
-                up = lax.dot_general(
-                    act, wu[r // NZ, r % NZ], (((1,), (1,)), ((), ())), preferred_element_type=F32
-                )
-                hout[rows, blk(r)] = (hbuf[rows, blk(r)].astype(F32) + up).astype(BF16)
-            f_copy(i).start()
-
-        @pl.when((s >= EARLY) & (s < NS - 1))
+            for q in range(NC):
+                for r in range(q * PER, (q + 1) * PER):
+                    up = lax.dot_general(
+                        act, w[r // NZ, r % NZ, 0:B], (((1,), (1,)), ((), ())), preferred_element_type=F32
+                    )
+                    hout[rows, blk(r)] = (hbuf[rows, blk(r)].astype(F32) + up).astype(BF16)
+                f_copy(i, q).start()
+
+        @pl.when((odd == 1) & (i == hand_at))
         def _():
-            @pl.when((s == EARLY) & (i == 1))
-            def _():
-                exchange_begin()
-
+            hand_on()
+
+        @pl.when(s < NS - 1)
+        def _():
+            pl.when(i == begin_at)(exchange_begin)
             for k, step in enumerate(exchange_steps):
-                pl.when(i == jnp.where(s == EARLY, k + 2, k))(step)
+                pl.when(i == begin_at + 1 + k)(step)
 
         return carry
 
     lax.fori_loop(0, NM, forward, 0)
 
+    @pl.when(begin_at >= NM)
+    def _():
+        exchange_begin()
+
     @pl.when(s < LATE)
     def _():
         start_gradient()
-
-    @pl.when(s < EARLY)
-    def _():
-        exchange_begin()
-        for step in exchange_steps:
-            step()
 
     @pl.when(s < NS - 1)
     def _():
         acc = jnp.zeros((TOK, R), F32)
         for r in range(NX * NZ):
-            acc = acc + jnp.dot(hout[:, blk(r)], wu[r // NZ, r % NZ], preferred_element_type=F32)
+            acc = acc + jnp.dot(hout[:, blk(r)], w[r // NZ, r % NZ, 0:B], preferred_element_type=F32)
         hup[...] = acc
+        for k, step in enumerate(exchange_steps):
+            pl.when(begin_at + 1 + k >= NM)(step)
 
     csum[...] = jnp.zeros((TOK, 128), F32)
 
-    def b_copy(j):
+    HT = TOK // 2
+
+    def b_copy(j, u):
+        part = msg.at[j, pl.ds(u * HT, HT)]
         return pltpu.make_async_remote_copy(
-            src_ref=msg.at[j], dst_ref=msg.at[j], send_sem=bsend.at[j], recv_sem=brecv.at[j],
+            src_ref=part, dst_ref=part, send_sem=bsend.at[j, u], recv_sem=brecv.at[j, u],
             device_id={"section": s_prev}, device_id_type=MESH,
         )
+
+    def receive(j, u):
+        b_copy(j, u).wait_recv()
+
+        @pl.when(s > 0)
+        def _():
+            b_copy(j, u).start()
+
+    def accumulate(j, rows):
+        c = msg[j, rows, 2 * R : 2 * R + 128].astype(F32)
+        csum[rows, :] += c
+        from_down = jnp.dot(
+            msg[j, rows, 0:R], mat[j, 0].reshape(R, R), preferred_element_type=F32
+        )
+        from_up = jnp.dot(
+            msg[j, rows, R : 2 * R], mat[j, 1].reshape(R, R), preferred_element_type=F32
+        )
+        both = jnp.concatenate([c, c], axis=1)
+        gacc[rows, :] += from_down + from_up - both * hup[rows, :]
 
     def arrive(t, carry):
         j = NS - 1 - t
-        b_copy(j).wait_recv()
+        for u in (0, 1):
+            receive(j, u)
+        accumulate(j, slice(0, TOK))
+        return carry
+
+    lax.fori_loop(0, NS - 2 - s, arrive, 0)
+
+    for u in (0, 1):
+        rows = slice(u * HT, (u + 1) * HT)
+
+        @pl.when(s < NS - 1)
+        def _(u=u, rows=rows):
+            receive(s + 1, u)
+            accumulate(s + 1, rows)
+
+        pre = prebuf[rows, :]
+        sig = jax.nn.sigmoid(pre)
+        inv = invbuf[rows, 0:1]
+        wide = gacc[rows, :] * sig * (1.0 + pre * (1.0 - sig))
+        scaled = (wide * inv).astype(BF16)
+        pgbuf[rows, :] = scaled
 
         @pl.when(s > 0)
-        def _():
-            b_copy(j).start()
-
-        c = msg[j, :, 2 * R : 2 * R + 128].astype(F32)
-        csum[...] += c
-        from_down = jnp.dot(
-            msg[j, :, 0:R], mat[j, 0].reshape(R, R), preferred_element_type=F32
-        )
-        from_up = jnp.dot(
-            msg[j, :, R : 2 * R], mat[j, 1].reshape(R, R), preferred_element_type=F32
-        )
-        both = jnp.concatenate([c, c], axis=1)
-        gacc[...] += from_down + from_up - both * hup[...]
-        return carry
-
-    lax.fori_loop(0, NS - 1 - s, arrive, 0)
-
-    pre = prebuf[...]
-    sig = jax.nn.sigmoid(pre)
-    pg = (gacc[...] * sig * (1.0 + pre * (1.0 - sig))).astype(BF16)
-    pgbuf[...] = pg
-
-    @pl.when(s > 0)
-    def _():
-        wide = pg.astype(F32)
-        inv = invbuf[:, 0:1]
-        coef = inv * inv * (jnp.sum(wide * pre, axis=-1, keepdims=True) * (1.0 / D))
-        msg[s, :, 0:R] = (wide * inv).astype(BF16)
-        msg[s, :, R : 2 * R] = (actbuf[...].astype(F32) * (-csum[:, 0:1])).astype(BF16)
-        msg[s, :, 2 * R : 2 * R + 128] = jnp.broadcast_to(coef, (TOK, 128)).astype(BF16)
-        b_copy(s).start()
+        def _(u=u, rows=rows, pre=pre, inv=inv, wide=wide, scaled=scaled):
+            coef = inv * inv * (jnp.sum(wide * pre, axis=-1, keepdims=True) * (1.0 / D))
+            msg[s, rows, 0:R] = scaled
+            msg[s, rows, R : 2 * R] = (actbuf[rows, :].astype(F32) * (-csum[rows, 0:1])).astype(BF16)
+            msg[s, rows, 2 * R : 2 * R + 128] = jnp.broadcast_to(coef, (HT, 128)).astype(BF16)
+            b_copy(s, u).start()
 
     pgt = pgbuf[...].astype(F32).T
     position = lax.broadcasted_iota(jnp.int32, (1, TOK), 1)
@@ -486,13 +551,16 @@
         masked[j * R : (j + 1) * R, :] = jnp.where(inside, pgt, 0.0).astype(BF16)
         start = end
 
-    for a in range(NX):
-        @pl.loop(0, NZ)
-        def _(b, a=a):
+    def square(count, where):
+        def one(t, carry):
+            a, b = where(t)
             cols = pl.ds(pl.multiple_of((a * NZ + b) * B, B), B)
             p = jnp.dot(masked[...], nbuf[:, cols], preferred_element_type=F32)
             p = p * p
             fsum[a, b] = (p[0:R] + p[R : 2 * R]) + (p[2 * R : 3 * R] + p[3 * R : 4 * R])
+            return carry
+
+        lax.fori_loop(0, count, one, 0)
 
     rcount = [0]
     rchan = {}
@@ -517,25 +585,23 @@
     def side(d):
         return 0 if d > 0 else 1
 
-    def part(d):
-        return slice(0, 64) if d > 0 else slice(64, 128)
-
-    HALF, FULL = pl.ds(0, 64), pl.ds(0, 128)
 
     def ring(key, axis, depth, mine, sbuf, rbuf, d, j):
         e = side(d)
+        value = mine(j * d)
+        m = value.shape[0] // 2
+        part = slice(0, m) if d > 0 else slice(m, 2 * m)
+        HALF, FULL = pl.ds(0, m), pl.ds(0, 2 * m)
         span = HALF if j == depth else FULL
-        value = mine(j * d)
         if j == depth:
-            sbuf[e, j - 1, 0:64] = value[part(d)].astype(BF16)
+            sbuf[e, j - 1, 0:m] = value[part].astype(BF16)
         else:
             if j == depth - 1:
                 r_copy(key + (d, j + 1), sbuf.at[e, j, HALF], rbuf.at[e, j, HALF], axis, d).wait_recv()
-                got = rbuf[e, j, 0:64].astype(F32)
-                fresh = part(d).start
-                keep = 64 - fresh
-                sbuf[e, j - 1, fresh : fresh + 64] = (value[part(d)] + got).astype(BF16)
-                sbuf[e, j - 1, keep : keep + 64] = value[keep : keep + 64].astype(BF16)
+                got = rbuf[e, j, 0:m].astype(F32)
+                keep = slice(m - part.start, 2 * m - part.start)
+                sbuf[e, j - 1, part] = (value[part] + got).astype(BF16)
+                sbuf[e, j - 1, keep] = value[keep].astype(BF16)
             else:
                 r_copy(key + (d, j + 1), sbuf.at[e, j, FULL], rbuf.at[e, j, FULL], axis, d).wait_recv()
                 sbuf[e, j - 1] = (value + rbuf[e, j].astype(F32)).astype(BF16)
@@ -543,6 +609,7 @@
 
     def ring_end(key, axis, mine, sbuf, rbuf):
         value = mine(0)
+        FULL = pl.ds(0, value.shape[0])
         for d in (1, -1):
             e = side(d)
             r_copy(key + (d, 1), sbuf.at[e, 0, FULL], rbuf.at[e, 0, FULL], axis, d).wait_recv()
@@ -550,23 +617,28 @@
         return value
 
     def stage_a(q, d, j):
-        ring(("A1", q), "x", 2, lambda k: fsum[xo(k), q, 0:128], ra_s.at[q], ra_r.at[q], d, j)
+        ring(("A1", q), "x", 2, lambda k: fsum[xo(k), q, 0:XROWS], ra_s.at[q], ra_r.at[q], d, j)
 
     def stage_b(c, d, j):
-        ring(("B1", c), "z", 4, lambda k: fsum[c, zo(k), 128:256], rb_s.at[c], rb_r.at[c], d, j)
-
+        ring(("B1", c), "z", 4, lambda k: fsum[c, zo(k), XROWS:R], rb_s.at[c], rb_r.at[c], d, j)
+
+    square(4, lambda t: (t, zo(4)))
     for c in range(NX):
         for d in (1, -1):
             stage_b(c, d, 4)
+    square(7, lambda t: (xo(2), zo(5 + t)))
     for q in range(NZ):
         for d in (1, -1):
             stage_a(q, d, 2)
+    square(6, lambda t: (xo(3 + lax.rem(t, 3)), zo(3 + 2 * (t // 3))))
     for c in range(NX):
         for d in (1, -1):
             stage_b(c, d, 3)
+    square(10, lambda t: (xo(1 + 2 * (t // 5)), zo(6 + lax.rem(t, 5))))
     for q in range(NZ):
         for d in (1, -1):
             stage_a(q, d, 1)
+    square(5, lambda t: (x, zo(6 + t)))
     for c in range(NX):
         for d in (1, -1):
             stage_b(c, d, 2)
@@ -574,7 +646,7 @@
         for d in (1, -1):
             stage_b(c, d, 1)
     for q in range(NZ):
-        ga[q] = ring_end(("A1", q), "x", lambda k: fsum[xo(k), q, 0:128], ra_s.at[q], ra_r.at[q])
+        ga[q] = ring_end(("A1", q), "x", lambda k: fsum[xo(k), q, 0:XROWS], ra_s.at[q], ra_r.at[q])
 
     def last_a(d, j):
         ring(("A2",), "z", 4, lambda k: ga[zo(k)], sa_s, sa_r, d, j)
@@ -585,7 +657,7 @@
     for d in (1, -1):
         last_a(d, 4)
     for c in range(NX):
-        gb[c] = ring_end(("B1", c), "z", lambda k: fsum[c, zo(k), 128:256], rb_s.at[c], rb_r.at[c])
+        gb[c] = ring_end(("B1", c), "z", lambda k: fsum[c, zo(k), XROWS:R], rb_s.at[c], rb_r.at[c])
     for d in (1, -1):
         last_b(d, 2)
     for d in (1, -1):
@@ -598,8 +670,7 @@
     low = ring_end(("A2",), "z", lambda k: ga[zo(k)], sa_s, sa_r)
     high = ring_end(("B2",), "x", lambda k: gb[xo(k)], sb_s, sb_r)
     scale = 1.0 / (TOK * NX * NZ)
-    out[0, :, 0:128] = low.T * scale
-    out[0, :, 128:256] = high.T * scale
+    out[0] = jnp.concatenate([low, high], axis=0).T * scale
     for c in sent:
         c.wait_send()
 
@@ -609,21 +680,31 @@
     def _():
         @pl.loop(0, NM)
         def _(i):
-            f_copy(i).wait_send()
+            for q in range(NC):
+                f_copy(i, q).wait_send()
 
     @pl.when(s > 0)
     def _():
         def done(t, carry):
-            b_copy(s + t).wait_send()
+            for u in (0, 1):
+                b_copy(s + t, u).wait_send()
             return carry
 
         lax.fori_loop(0, NS - s, done, 0)
 
+        @pl.when(odd == 1)
+        def _():
+            e_copy(s, s - 1).wait_send()
+
         def offered(t, carry):
-            e_copy(s, t).wait_send()
+            e_copy(s, s - 1 - odd - 2 * t).wait_send()
             return carry
 
-        lax.fori_loop(0, s, offered, 0)
+        lax.fori_loop(0, s // 2, offered, 0)
+
+    @pl.when(odd == 1)
+    def _():
+        handed()
 
 
 def per_device(tokens, cotangent, down_weight, up_weight, norm_gain, lengths):
@@ -636,8 +717,7 @@
         in_specs=[hbm, hbm, hbm, hbm, vmem, pl.BlockSpec(memory_space=pltpu.SMEM)],
         out_specs=vmem,
         scratch_shapes=[
-            pltpu.VMEM((NX, NZ, B, R), BF16),
-            pltpu.VMEM((NX, NZ, B, R), BF16),
+            pltpu.VMEM((NX, NZ, 2 * B, R), BF16),
             pltpu.VMEM((TOK, D), BF16),
             pltpu.VMEM((TOK, D), BF16),
             pltpu.VMEM((TOK, D), BF16),
@@ -654,23 +734,24 @@
             pltpu.VMEM((TOK, R), BF16),
             pltpu.VMEM((4 * R, TOK), BF16),
             pltpu.VMEM((NX, NZ, R, B), F32),
-            pltpu.VMEM((NX, 2, 4, 128, B), BF16),
-            pltpu.VMEM((NX, 2, 4, 128, B), BF16),
-            pltpu.VMEM((NZ, 2, 2, 128, B), BF16),
-            pltpu.VMEM((NZ, 2, 2, 128, B), BF16),
-            pltpu.VMEM((NX, 128, B), F32),
-            pltpu.VMEM((NZ, 128, B), F32),
-            pltpu.VMEM((2, 2, 128, B), BF16),
-            pltpu.VMEM((2, 2, 128, B), BF16),
-            pltpu.VMEM((2, 4, 128, B), BF16),
-            pltpu.VMEM((2, 4, 128, B), BF16),
+            pltpu.VMEM((NX, 2, 4, R - XROWS, B), BF16),
+            pltpu.VMEM((NX, 2, 4, R - XROWS, B), BF16),
+            pltpu.VMEM((NZ, 2, 2, XROWS, B), BF16),
+            pltpu.VMEM((NZ, 2, 2, XROWS, B), BF16),
+            pltpu.VMEM((NX, R - XROWS, B), F32),
+            pltpu.VMEM((NZ, XROWS, B), F32),
+            pltpu.VMEM((2, 2, R - XROWS, B), BF16),
+            pltpu.VMEM((2, 2, R - XROWS, B), BF16),
+            pltpu.VMEM((2, 4, XROWS, B), BF16),
+            pltpu.VMEM((2, 4, XROWS, B), BF16),
             dma((4,)),
             dma((GATHER_CHANNELS,)),
             dma((GATHER_CHANNELS,)),
-            dma((NM,)),
-            dma((NS,)),
+            dma((NM, NC)),
+            dma((NS, 2)),
             dma((RS_CHANNELS,)),
-            dma((NM,)),
+            dma((NM, NC)),
+            dma((NS, 2)),
             dma((NS,)),
             dma((NS,)),
             dma((NS,)),

time: 194 us -> 179 us (0.923)
  Pallas kernels: 192 us -> 177 us
    pallas_call x1, Pallas kernels: 192 us -> 177 us  [per_device(): pl.pallas_call(kernel, out_shape=jax.ShapeDtypeStruct((1, B, R), F32), in...]
where the time goes in v3:
time: 179 us; the launch traced here: 178 us
  Pallas kernels  177 us (99%)
    pallas_call x1, Pallas kernels, per_device(): pl.pallas_call(kernel, out_shape=jax.ShapeDtypeStruct((1, B, R), F32), in...  177 us

profile of v3, /device:TPU:32, one launch (start us, length us, event | category | flops | bytes accessed | tf_op | source)
XLA Modules:
  0.0 178.5 jit_solution(9371165414857920940)
XLA Ops:
  0.0 176.8 %shard_map.64 = f32[1,256,256]{2,1,0:T(8,128)} custom-call(bf16[128,8192]{1,0:T(8,128)(2,1)} %tok.1, bf16[128,8192]{1,0:T(8,128)(2,1)} %cot.1, bf16[256,256]{1,0:T(8,128)(2,1)} %bitcast.2, bf16[256,256]{1,0:T(8,128)(2,1)} %bitcast.3, f32[1,8192]{1,0:T(1,128)} %gain.1, s32[1,4]{1,0:T(1,128)} %lens.1), custom_call_target="tpu_custom_call" | custom-call | tf_op jit(solution)/shard_map/pallas_call | solution.py:714
  176.8 1.7 copy.8

commit v4 on v3

--- a/solution.py
+++ b/solution.py
@@ -237,7 +237,7 @@
         first.wait()
 
     LATE = 4
-    begin_at = jnp.where(s >= 5, -1, jnp.where(s == 4, 1, jnp.where(s == 3, 5, jnp.where(s == 2, 6, NM))))
+    begin_at = jnp.where(s >= 5, -1, jnp.where(s == 4, 5, jnp.where(s == 3, 5, jnp.where(s == 2, 6, NM))))
     hand_at = jnp.where(s >= 5, -1, jnp.where(s == 3, 4, NM - 1))
 
     def blk(r):

time: 179 us -> 177 us (0.989)
  Pallas kernels: 177 us -> 175 us
where the time goes in v4:
time: 177 us
  Pallas kernels  175 us (99%)
    pallas_call x1, Pallas kernels, per_device(): pl.pallas_call(kernel, out_shape=jax.ShapeDtypeStruct((1, B, R), F32), in...  175 us

profile of v4, /device:TPU:32, one launch (start us, length us, event | category | flops | bytes accessed | tf_op | source)
XLA Modules:
  0.0 176.8 jit_solution(12828621195919686204)
XLA Ops:
  0.0 175.1 %shard_map.64 = f32[1,256,256]{2,1,0:T(8,128)} custom-call(bf16[128,8192]{1,0:T(8,128)(2,1)} %tok.1, bf16[128,8192]{1,0:T(8,128)(2,1)} %cot.1, bf16[256,256]{1,0:T(8,128)(2,1)} %bitcast.2, bf16[256,256]{1,0:T(8,128)(2,1)} %bitcast.3, f32[1,8192]{1,0:T(1,128)} %gain.1, s32[1,4]{1,0:T(1,128)} %lens.1), custom_call_target="tpu_custom_call" | custom-call | tf_op jit(solution)/shard_map/pallas_call | solution.py:714
  175.2 1.7 copy.8

commit v5 on v4

--- a/solution.py
+++ b/solution.py
@@ -237,8 +237,8 @@
         first.wait()
 
     LATE = 4
-    begin_at = jnp.where(s >= 5, -1, jnp.where(s == 4, 5, jnp.where(s == 3, 5, jnp.where(s == 2, 6, NM))))
-    hand_at = jnp.where(s >= 5, -1, jnp.where(s == 3, 4, NM - 1))
+    begin_at = jnp.where(s >= 5, -1, jnp.where(s == 4, 5, jnp.where(s == 3, 7, NM)))
+    hand_at = jnp.where(s >= 5, -1, jnp.where(s == 3, 6, NM - 1))
 
     def blk(r):
         return slice(r * B, (r + 1) * B)

time: 177 us -> 177 us (level)
  no operation moved by 1% of the time
where the time goes in v5:
time: 177 us
  Pallas kernels  175 us (99%)
    pallas_call x1, Pallas kernels, per_device(): pl.pallas_call(kernel, out_shape=jax.ShapeDtypeStruct((1, B, R), F32), in...  175 us

profile of v5, /device:TPU:32, one launch (start us, length us, event | category | flops | bytes accessed | tf_op | source)
XLA Modules:
  0.0 176.8 jit_solution(6219563354328178019)
XLA Ops:
  0.0 175.1 %shard_map.64 = f32[1,256,256]{2,1,0:T(8,128)} custom-call(bf16[128,8192]{1,0:T(8,128)(2,1)} %tok.1, bf16[128,8192]{1,0:T(8,128)(2,1)} %cot.1, bf16[256,256]{1,0:T(8,128)(2,1)} %bitcast.2, bf16[256,256]{1,0:T(8,128)(2,1)} %bitcast.3, f32[1,8192]{1,0:T(1,128)} %gain.1, s32[1,4]{1,0:T(1,128)} %lens.1), custom_call_target="tpu_custom_call" | custom-call | tf_op jit(solution)/shard_map/pallas_call | solution.py:714
  175.2 1.7 copy.8
